TPU v7x, 32 devices: a whole 2x2x4 slice. The times are simulated.
32 devices in a mesh: dp: 8 (over z, y), head: 4 (over x, core).
Axes of the slice: x: 2, y: 2, z: 4, core: 2. Of those that a mesh axis runs over, the one named last changes fastest.
Arguments:
- inputs: bfloat16 [16, 2048, 768], P('dp', 'head'), may hold values from -6 to 6
- lengths: int32 [16], P('dp'), may hold values from 1 to 2048, 24576 in all
- w_query: bfloat16 [768, 768], P('head'), may hold values from -0.21875 to 0.21875
- w_key: bfloat16 [768, 768], P('head'), may hold values from -0.21875 to 0.21875
- w_value: bfloat16 [768, 768], P('head'), may hold values from -0.21875 to 0.21875
- w_out: bfloat16 [768, 768], P('head'), may hold values from -1.75 to 1.75
- w_up: bfloat16 [768, 3072], P(None, 'head'), may hold values from -0.21875 to 0.21875
- w_down: bfloat16 [3072, 768], P('head'), may hold values from -0.109375 to 0.109375
- conv_taps: bfloat16 [3, 3, 768], P(None, None, 'head'), may hold values from -3.5 to 3.5
- gain_attn: bfloat16 [768], replicated, may hold values from 0.5 to 1.5
- gain_ff: bfloat16 [768], replicated, may hold values from 0.5 to 1.5
- cotangent: bfloat16 [16, 2048, 768], P('dp', 'head'), may hold values from -6 to 6
Outputs:
- output: float32 [16, 2048, 768], P('dp', 'head')
- grad_input: float32 [16, 2048, 768], P('dp', 'head')
- grad_query: float32 [768, 768], P('head')
- grad_key: float32 [768, 768], P('head')
- grad_value: float32 [768, 768], P('head')
- grad_out: float32 [768, 768], P('head')
- grad_up: float32 [768, 3072], P(None, 'head')
- grad_down: float32 [3072, 768], P('head')
- grad_taps: float32 [3, 3, 768], P(None, None, 'head')
- grad_gain_attn: float32 [768], P('head')
- grad_gain_ff: float32 [768], P('head')
Inputs may be any that keep to these rules, and one draw needn't show every extreme that they name: `lengths`: one sequence in every draw has all 2048 positions real.
All inputs are finite; a program needn't handle non-finite values. No bound on the sum of `lengths` on one device may be relied on, other than what follows from the above.
Results may differ from a plain program's by a relative error of at most 0.015.
The roundings to bfloat16 on the way count: a program that leaves them out, or rounds other values in their place, can miss the bound.
Values may be sent and summed in bfloat16 or wider, within the bound.
No kernel may reach another device: no remote copies, remote signals or barrier semaphores. Data moves between devices by JAX's collectives and lax.ppermute only.
A program may use at most 256 MiB of HBM per device.

v0:
```python
import jax
import jax.numpy as jnp
from jax import lax
from jax.sharding import PartitionSpec as P

HDIM = 64


epsilon = 1e-06


def lead_sum(values):
    return jnp.sum(values, axis=tuple(range(values.ndim - 1)))


def rms_parts(values, gain_vec):
    inverse = lax.rsqrt(jnp.mean(values * values, axis=-1, keepdims=True) + epsilon)
    scaled = values * inverse
    return (scaled, inverse, (scaled * gain_vec).astype(jnp.bfloat16))


def rms_back(grad_normed, scaled, inverse, gain_vec):
    grad_gain = lead_sum(grad_normed * scaled)
    grad_scaled = grad_normed * gain_vec
    grad_values = inverse * (
        grad_scaled - scaled * jnp.mean(grad_scaled * scaled, axis=-1, keepdims=True)
    )
    return (grad_values, grad_gain)


def conv_forward(values, conv_row):
    length = values.shape[0]
    padded = jnp.concatenate([jnp.zeros((2, values.shape[1]), jnp.float32), values], axis=0)
    return (
        conv_row[0] * values + conv_row[1] * padded[1 : length + 1] + conv_row[2] * padded[0:length]
    )


def conv_backward(grad_mixed, values, conv_row):
    length = values.shape[0]
    blank = jnp.zeros((2, values.shape[1]), jnp.float32)
    grad_padded = jnp.concatenate([grad_mixed, blank], axis=0)
    value_padded = jnp.concatenate([blank, values], axis=0)
    grad_values = (
        conv_row[0] * grad_mixed
        + conv_row[1] * grad_padded[1 : length + 1]
        + conv_row[2] * grad_padded[2 : length + 2]
    )
    grad_row = jnp.stack(
        [
            jnp.sum(grad_mixed * values, axis=0),
            jnp.sum(grad_mixed * value_padded[1 : length + 1], axis=0),
            jnp.sum(grad_mixed * value_padded[0:length], axis=0),
        ],
        axis=0,
    )
    return (grad_values, grad_row)


def allowed_mask(block_start, block_rows, length, seq_limit):
    key_place = jnp.arange(length)
    query_place = block_start + jnp.arange(block_rows)
    return (key_place[None, :] <= query_place[:, None]) & (key_place[None, :] < seq_limit)


def attention_forward(queries, key_rows, value_rows, seq_limit):
    length = queries.shape[0]
    block_rows = min(512, length)
    score_scale = HDIM ** (-0.5)

    def one_block(block_start):
        query_rows = lax.dynamic_slice_in_dim(queries, block_start, block_rows, 0)
        scores = (
            jnp.einsum("qhd,khd->hqk", query_rows, key_rows, preferred_element_type=jnp.float32)
            * score_scale
        )
        allowed = allowed_mask(block_start, block_rows, length, seq_limit)
        masked = jnp.where(allowed[None], scores, -1000000000.0)
        row_top = jnp.max(masked, axis=-1, keepdims=True)
        raised = jnp.where(allowed[None], jnp.exp(masked - row_top), 0.0)
        row_total = jnp.sum(raised, axis=-1, keepdims=True)
        weights_low = (raised / row_total).astype(jnp.bfloat16)
        result = jnp.einsum(
            "hqk,khd->qhd", weights_low, value_rows, preferred_element_type=jnp.float32
        )
        return (result, row_top + jnp.log(row_total))

    block_starts = jnp.arange(length // block_rows) * block_rows
    results, log_sums = lax.map(one_block, block_starts)
    return (results.reshape(queries.shape), log_sums)


def attention_backward(queries, key_rows, value_rows, grad_heads, log_sums, seq_limit):
    length = queries.shape[0]
    block_rows = min(512, length)
    score_scale = HDIM ** (-0.5)

    def one_block(carry, pieces):
        grad_keys, grad_values = carry
        block_start, log_sum = pieces
        query_rows = lax.dynamic_slice_in_dim(queries, block_start, block_rows, 0)
        grad_rows = lax.dynamic_slice_in_dim(grad_heads, block_start, block_rows, 0)
        scores = (
            jnp.einsum("qhd,khd->hqk", query_rows, key_rows, preferred_element_type=jnp.float32)
            * score_scale
        )
        allowed = allowed_mask(block_start, block_rows, length, seq_limit)
        masked = jnp.where(allowed[None], scores, -1000000000.0)
        probs = jnp.where(allowed[None], jnp.exp(masked - log_sum), 0.0)
        grad_probs = jnp.einsum(
            "qhd,khd->hqk", grad_rows, value_rows, preferred_element_type=jnp.float32
        )
        grad_scores = probs * (grad_probs - jnp.sum(probs * grad_probs, axis=-1, keepdims=True))
        grad_low = grad_scores.astype(jnp.bfloat16)
        grad_query = (
            jnp.einsum("hqk,khd->qhd", grad_low, key_rows, preferred_element_type=jnp.float32)
            * score_scale
        )
        grad_keys = (
            grad_keys
            + jnp.einsum("hqk,qhd->khd", grad_low, query_rows, preferred_element_type=jnp.float32)
            * score_scale
        )
        grad_values = grad_values + jnp.einsum(
            "hqk,qhd->khd",
            probs.astype(jnp.bfloat16),
            grad_rows,
            preferred_element_type=jnp.float32,
        )
        return ((grad_keys, grad_values), grad_query)

    block_starts = jnp.arange(length // block_rows) * block_rows
    zeros_start = jnp.zeros(key_rows.shape, jnp.float32)
    (grad_keys, grad_values), grad_queries = lax.scan(
        one_block, (zeros_start, zeros_start), (block_starts, log_sums)
    )
    return (grad_queries.reshape(queries.shape), grad_keys, grad_values)


def local(
    inputs,
    lengths,
    w_query,
    w_key,
    w_value,
    w_out,
    w_up,
    w_down,
    conv_taps,
    gain_attn,
    gain_ff,
    cotangent,
):
    groups = lax.axis_size("head")
    seq_count = inputs.shape[0]
    row_count = inputs.shape[1]
    model_width = inputs.shape[2]
    length = row_count * groups
    channels = model_width // groups
    heads_here = channels // HDIM
    stream = inputs.astype(jnp.float32)
    positions = lax.axis_index("head") * row_count + jnp.arange(row_count)
    row_valid = (positions[None, :] < lengths[:, None])[:, :, None]
    gain_one = gain_attn.astype(jnp.float32)
    gain_two = gain_ff.astype(jnp.float32)
    conv_weights = conv_taps.astype(jnp.float32)
    full_query, full_key, full_value, full_out = (
        lax.all_gather(w_query, "head", axis=0, tiled=True),
        lax.all_gather(w_key, "head", axis=0, tiled=True),
        lax.all_gather(w_value, "head", axis=0, tiled=True),
        lax.all_gather(w_out, "head", axis=0, tiled=True),
    )
    full_proj = jnp.stack([full_query, full_key, full_value], axis=0)
    scaled_one, inverse_one, normed = rms_parts(stream, gain_one)
    projected = jnp.einsum(
        "srd,kde->srke", normed, full_proj, preferred_element_type=jnp.float32
    ).astype(jnp.bfloat16)
    head_side = lax.all_to_all(
        projected.reshape(seq_count, row_count, 3, groups, channels),
        "head",
        split_axis=3,
        concat_axis=1,
        tiled=True,
    )
    projected_raw = head_side.reshape(seq_count, length, 3, channels).astype(jnp.float32)
    conv_many = jax.vmap(conv_forward, in_axes=(0, None))
    mixed_low = [
        conv_many(projected_raw[:, :, which], conv_weights[which])
        .astype(jnp.bfloat16)
        .reshape(seq_count, length, heads_here, HDIM)
        for which in range(3)
    ]
    attended, log_sums = jax.vmap(attention_forward)(
        mixed_low[0], mixed_low[1], mixed_low[2], lengths
    )
    attended_low = attended.reshape(seq_count, length, 1, channels).astype(jnp.bfloat16)
    token_side = lax.all_to_all(
        attended_low, "head", split_axis=1, concat_axis=2, tiled=True
    ).reshape(seq_count, row_count, model_width)
    middle = stream + jnp.einsum(
        "src,cd->srd", token_side, full_out, preferred_element_type=jnp.float32
    )
    scaled_two, inverse_two, normed_ff = rms_parts(middle, gain_two)
    whole_up, whole_down = (
        lax.all_gather(w_up, "head", axis=1, tiled=True),
        lax.all_gather(w_down, "head", axis=0, tiled=True),
    )
    hidden_pre = jnp.einsum("srd,df->srf", normed_ff, whole_up, preferred_element_type=jnp.float32)
    hidden = jnp.square(jax.nn.relu(hidden_pre)).astype(jnp.bfloat16)
    ff_out = jnp.einsum("srf,fd->srd", hidden, whole_down, preferred_element_type=jnp.float32)
    output = jnp.where(row_valid, middle + ff_out, 0.0)
    grad_res = jnp.where(row_valid, cotangent.astype(jnp.float32), 0.0)
    grad_ff = grad_res.astype(jnp.bfloat16)
    grad_hidden = jnp.einsum("srd,fd->srf", grad_ff, whole_down, preferred_element_type=jnp.float32)
    grad_pre = (grad_hidden * 2.0 * jax.nn.relu(hidden_pre)).astype(jnp.bfloat16)
    grad_down_part = jnp.einsum("srf,srd->fd", hidden, grad_ff, preferred_element_type=jnp.float32)
    grad_up_part = jnp.einsum(
        "srd,srf->df", normed_ff, grad_pre, preferred_element_type=jnp.float32
    )
    grad_normed_ff = jnp.einsum(
        "srf,df->srd", grad_pre, whole_up, preferred_element_type=jnp.float32
    )
    grad_up_local, grad_down_local = (
        lax.psum_scatter(grad_up_part, "head", scatter_dimension=1, tiled=True),
        lax.psum_scatter(grad_down_part, "head", scatter_dimension=0, tiled=True),
    )
    grad_mid_norm, grad_gain_two = rms_back(grad_normed_ff, scaled_two, inverse_two, gain_two)
    grad_middle = grad_res + grad_mid_norm
    grad_branch = grad_middle.astype(jnp.bfloat16)
    grad_out_part = jnp.einsum(
        "src,srd->cd", token_side, grad_branch, preferred_element_type=jnp.float32
    )
    grad_attended = jnp.einsum(
        "srd,cd->src", grad_branch, full_out, preferred_element_type=jnp.float32
    ).astype(jnp.bfloat16)
    grad_heads = lax.all_to_all(
        grad_attended.reshape(seq_count, row_count, groups, channels),
        "head",
        split_axis=2,
        concat_axis=1,
        tiled=True,
    )
    grad_heads = grad_heads.reshape(seq_count, length, heads_here, HDIM)
    grad_queries, grad_keys, grad_values = jax.vmap(attention_backward)(
        mixed_low[0], mixed_low[1], mixed_low[2], grad_heads, log_sums, lengths
    )
    conv_back_many = jax.vmap(conv_backward, in_axes=(0, 0, None))
    conv_results = [
        conv_back_many(
            grad_item.reshape(seq_count, length, channels),
            projected_raw[:, :, which],
            conv_weights[which],
        )
        for which, grad_item in enumerate((grad_queries, grad_keys, grad_values))
    ]
    grad_raw = jnp.stack([item[0] for item in conv_results], axis=2).astype(jnp.bfloat16)
    grad_conv = jnp.stack([jnp.sum(item[1], axis=0) for item in conv_results], axis=0)
    back_tokens = lax.all_to_all(
        grad_raw.reshape(seq_count, length, 3, 1, channels),
        "head",
        split_axis=1,
        concat_axis=3,
        tiled=True,
    )
    back_tokens = back_tokens.reshape(seq_count, row_count, 3, model_width)
    grad_proj_parts = jnp.einsum(
        "srd,srke->kde", normed, back_tokens, preferred_element_type=jnp.float32
    )
    grad_normed = jnp.einsum(
        "srke,kde->srd", back_tokens, full_proj, preferred_element_type=jnp.float32
    )
    grad_in_norm, grad_gain_one = rms_back(grad_normed, scaled_one, inverse_one, gain_one)
    head_query, head_key, head_value, head_out, head_gain_one, head_gain_two = (
        lax.psum_scatter(grad_proj_parts[0], "head", scatter_dimension=0, tiled=True),
        lax.psum_scatter(grad_proj_parts[1], "head", scatter_dimension=0, tiled=True),
        lax.psum_scatter(grad_proj_parts[2], "head", scatter_dimension=0, tiled=True),
        lax.psum_scatter(grad_out_part, "head", scatter_dimension=0, tiled=True),
        lax.psum_scatter(grad_gain_one, "head", scatter_dimension=0, tiled=True),
        lax.psum_scatter(grad_gain_two, "head", scatter_dimension=0, tiled=True),
    )
    grad_input = grad_middle + grad_in_norm
    summed = lax.psum(
        (
            head_query,
            head_key,
            head_value,
            head_out,
            grad_up_local,
            grad_down_local,
            grad_conv,
            head_gain_one,
            head_gain_two,
        ),
        "dp",
    )
    return (
        output,
        grad_input,
        summed[0],
        summed[1],
        summed[2],
        summed[3],
        summed[4],
        summed[5],
        summed[6],
        summed[7],
        summed[8],
    )


def solution(mesh):
    placed = (
        P("dp", "head", None),
        P("dp"),
        P("head", None),
        P("head", None),
        P("head", None),
        P("head", None),
        P(None, "head"),
        P("head", None),
        P(None, None, "head"),
        P(),
        P(),
        P("dp", "head", None),
    )
    return jax.shard_map(
        local,
        mesh=mesh,
        in_specs=placed,
        out_specs=(
            P("dp", "head", None),
            P("dp", "head", None),
            P("head", None),
            P("head", None),
            P("head", None),
            P("head", None),
            P(None, "head"),
            P("head", None),
            P(None, None, "head"),
            P("head"),
            P("head"),
        ),
        check_vma=False,
    )
```

profile of v0, /device:TPU:0, one launch (start us, length us, event | category | flops | bytes accessed | tf_op | source)
XLA Modules:
  0.0 1708.3 jit_solution(11550276693208969229)
XLA Ops:
  11.7 18.1 %all-gather.7.cloned.1.call-done = bf16[768,768]{1,0:T(8,128)(2,1)} async-done(((bf16[192,768]{1,0:T(8,128)(2,1)}), bf16[768,768]{1,0:T(8,128)(2,1)}) %all-gather.7.cloned.1.call-update) | async-done | bytes 1179664 | tf_op jit(solution)/shard_map/all_gather | solution.py:168
  29.8 19.1 %all-gather.9.cloned.1.call-done = bf16[768,768]{1,0:T(8,128)(2,1)} async-done(((bf16[192,768]{1,0:T(8,128)(2,1)}), bf16[768,768]{1,0:T(8,128)(2,1)}) %all-gather.9.cloned.1.call-update) | async-done | bytes 1179664 | tf_op jit(solution)/shard_map/all_gather | solution.py:169
  48.8 19.1 %all-gather.11.cloned.1.call-done = bf16[768,768]{1,0:T(8,128)(2,1)} async-done(((bf16[192,768]{1,0:T(8,128)(2,1)}), bf16[768,768]{1,0:T(8,128)(2,1)}) %all-gather.11.cloned.1.call-update) | async-done | bytes 1179664 | tf_op jit(solution)/shard_map/all_gather | solution.py:170
  93.4 87.3 %all-to-all-done = bf16[2,512,3,4,192]{1,4,2,0,3:T(8,128)(2,1)} async-done(((bf16[2,512,3,4,192]{1,4,2,0,3:T(8,128)(2,1)}), bf16[2,512,3,4,192]{1,4,2,0,3:T(8,128)(2,1)}, u32[]{:S(2)}, u32[]{:S(2)}) %all-to-all-start) | async-done | bytes 4718624 | tf_op jit(solution)/shard_map/all_to_all | solution.py:178
  188.1 13.4 copy.69
  201.5 12.6 reshape.418
  236.1 177.4 %while.30 = (s32[]{:T(128)}, bf16[4,2,512,3,64]{2,4,3,1,0:T(8,128)(2,1)}, f32[4,2,3,512,1]{3,2,1,4,0:T(4,128)S(1)}, s32[4]{0:T(128)S(1)}, s32[2]{0:T(128)S(1)}, ...) while((s32[]{:T(128)}, ...), condition=%wide.region_4.5_spmd, body=%wide.region_1.4_spmd.sunk | while | flops 1701840384 | bytes 103022848 | solution.py:89
  241.8 12.3 fusion.111
  254.1 12.5 fusion.112
  266.6 13.1 fusion.113
  286.1 12.3 fusion.111
  298.4 12.5 fusion.112
  310.8 13.1 fusion.113
  330.3 12.3 fusion.111
  342.6 12.5 fusion.112
  355.1 13.1 fusion.113
  386.8 12.5 fusion.112
  399.3 13.1 fusion.113
  432.3 25.5 %all-to-all-done.1 = bf16[2,2048,1,192]{3,0,2,1:T(2,128)(2,1)S(1)} async-done(((bf16[2,2048,1,192]{3,0,2,1:T(2,128)(2,1)}), bf16[2,2048,1,192]{3,0,2,1:T(2,128)(2,1)S(1)}, u32[]{:S(2)}, u32[]{:S(2)}) %all-to-all-start.1) | async-done | bytes 1572896 | tf_op jit(solution)/shard_map/all_to_all | solution.py:197
  511.7 20.1 %all-to-all-done.2 = bf16[2,512,4,192]{1,3,0,2:T(8,128)(2,1)} async-done(((bf16[2,512,4,192]{1,3,0,2:T(8,128)(2,1)}), bf16[2,512,4,192]{1,3,0,2:T(8,128)(2,1)}, u32[]{:S(2)}, u32[]{:S(2)}) %all-to-all-start.2) | async-done | bytes 1572896 | tf_op jit(solution)/shard_map/all_to_all | solution.py:236
  539.4 432.1 %while.31 = (s32[]{:T(128)}, f32[2,2048,3,64]{1,3,2,0:T(8,128)S(1)}, f32[2,2048,3,64]{1,3,2,0:T(8,128)}, f32[4,2,512,3,64]{2,0,4,3,1:T(4,128)}, s32[4]{0:T(128)S...) while((s32[]{:T(128)}, ...), condition=%wide.region_9.10_spmd.clone, body=%wide.region_7.9_spmd.clone.sunk | while | flops 4096722432 | bytes 227352864 | solution.py:134
  557.7 20.5 %multiply_reduce_fusion.14 = (f32[2,3,512]{2,1,0:T(4,128)S(1)}, f32[2,3,512,2048]{3,2,1,0:T(8,128)}) fusion(f32[2,3,512,2048]{3,2,1,0:T(8,128)} %fusion.123, f32[2,3,512]{2,1,0:T(4,128)S(1)} %dynamic-slice_bitcast_fusion.2, bf16[2,2048,3,64]{1,3,2,0:T(8,128)(2,1)} %get-tuple-element.516, bf16[2,2048,3,64]{1,3,2,0:T(8,128)(2,1)} %get-tuple-element.514, ...), kind=kOutput, calls=%fused_computation.21.clone.1 | convolution fusion | flops 843052032 | bytes 54419460 | tf_op jit(solution)/shard_map/vmap()/while/body/eval_jaxpr/qhd,khd->hqk/dot_general | solution.py:104
  578.2 21.1 %multiply_convert_fusion.9 = bf16[2,3,512,2048]{3,2,1,0:T(8,128)(2,1)} fusion(f32[2,3,512,2048]{3,2,1,0:T(8,128)} %get-tuple-element.446, f32[2,3,512,2048]{3,2,1,0:T(8,128)} %fusion.123, f32[2,3,512]{2,1,0:T(4,128)S(1)} %get-tuple-element.447), kind=kLoop, calls=%fused_computation.20.clone.1 | loop fusion | flops 18874368 | bytes 62926848 | tf_op jit(solution)/shard_map/vmap()/while/body/eval_jaxpr/convert_element_type | solution.py:114
  599.3 12.5 bitcast_add_fusion.5
  630.9 16.1 dynamic_update_slice.19
  664.9 20.5 %multiply_reduce_fusion.14 = (f32[2,3,512]{2,1,0:T(4,128)S(1)}, f32[2,3,512,2048]{3,2,1,0:T(8,128)}) fusion(f32[2,3,512,2048]{3,2,1,0:T(8,128)} %fusion.123, f32[2,3,512]{2,1,0:T(4,128)S(1)} %dynamic-slice_bitcast_fusion.2, bf16[2,2048,3,64]{1,3,2,0:T(8,128)(2,1)} %get-tuple-element.516, bf16[2,2048,3,64]{1,3,2,0:T(8,128)(2,1)} %get-tuple-element.514, ...), kind=kOutput, calls=%fused_computation.21.clone.1 | convolution fusion | flops 843052032 | bytes 54419460 | tf_op jit(solution)/shard_map/vmap()/while/body/eval_jaxpr/qhd,khd->hqk/dot_general | solution.py:104
  685.4 21.1 %multiply_convert_fusion.9 = bf16[2,3,512,2048]{3,2,1,0:T(8,128)(2,1)} fusion(f32[2,3,512,2048]{3,2,1,0:T(8,128)} %get-tuple-element.446, f32[2,3,512,2048]{3,2,1,0:T(8,128)} %fusion.123, f32[2,3,512]{2,1,0:T(4,128)S(1)} %get-tuple-element.447), kind=kLoop, calls=%fused_computation.20.clone.1 | loop fusion | flops 18874368 | bytes 62926848 | tf_op jit(solution)/shard_map/vmap()/while/body/eval_jaxpr/convert_element_type | solution.py:114
  706.6 13.3 bitcast_add_fusion.5
  739.0 16.1 dynamic_update_slice.19
  773.1 20.5 %multiply_reduce_fusion.14 = (f32[2,3,512]{2,1,0:T(4,128)S(1)}, f32[2,3,512,2048]{3,2,1,0:T(8,128)}) fusion(f32[2,3,512,2048]{3,2,1,0:T(8,128)} %fusion.123, f32[2,3,512]{2,1,0:T(4,128)S(1)} %dynamic-slice_bitcast_fusion.2, bf16[2,2048,3,64]{1,3,2,0:T(8,128)(2,1)} %get-tuple-element.516, bf16[2,2048,3,64]{1,3,2,0:T(8,128)(2,1)} %get-tuple-element.514, ...), kind=kOutput, calls=%fused_computation.21.clone.1 | convolution fusion | flops 843052032 | bytes 54419460 | tf_op jit(solution)/shard_map/vmap()/while/body/eval_jaxpr/qhd,khd->hqk/dot_general | solution.py:104
  793.6 21.1 %multiply_convert_fusion.9 = bf16[2,3,512,2048]{3,2,1,0:T(8,128)(2,1)} fusion(f32[2,3,512,2048]{3,2,1,0:T(8,128)} %get-tuple-element.446, f32[2,3,512,2048]{3,2,1,0:T(8,128)} %fusion.123, f32[2,3,512]{2,1,0:T(4,128)S(1)} %get-tuple-element.447), kind=kLoop, calls=%fused_computation.20.clone.1 | loop fusion | flops 18874368 | bytes 62926848 | tf_op jit(solution)/shard_map/vmap()/while/body/eval_jaxpr/convert_element_type | solution.py:114
  814.7 13.3 bitcast_add_fusion.5
  847.2 16.1 dynamic_update_slice.19
  881.2 20.5 %multiply_reduce_fusion.14 = (f32[2,3,512]{2,1,0:T(4,128)S(1)}, f32[2,3,512,2048]{3,2,1,0:T(8,128)}) fusion(f32[2,3,512,2048]{3,2,1,0:T(8,128)} %fusion.123, f32[2,3,512]{2,1,0:T(4,128)S(1)} %dynamic-slice_bitcast_fusion.2, bf16[2,2048,3,64]{1,3,2,0:T(8,128)(2,1)} %get-tuple-element.516, bf16[2,2048,3,64]{1,3,2,0:T(8,128)(2,1)} %get-tuple-element.514, ...), kind=kOutput, calls=%fused_computation.21.clone.1 | convolution fusion | flops 843052032 | bytes 54419460 | tf_op jit(solution)/shard_map/vmap()/while/body/eval_jaxpr/qhd,khd->hqk/dot_general | solution.py:104
  901.7 21.1 %multiply_convert_fusion.9 = bf16[2,3,512,2048]{3,2,1,0:T(8,128)(2,1)} fusion(f32[2,3,512,2048]{3,2,1,0:T(8,128)} %get-tuple-element.446, f32[2,3,512,2048]{3,2,1,0:T(8,128)} %fusion.123, f32[2,3,512]{2,1,0:T(4,128)S(1)} %get-tuple-element.447), kind=kLoop, calls=%fused_computation.20.clone.1 | loop fusion | flops 18874368 | bytes 62926848 | tf_op jit(solution)/shard_map/vmap()/while/body/eval_jaxpr/convert_element_type | solution.py:114
  922.8 13.3 bitcast_add_fusion.5
  955.2 16.1 dynamic_update_slice.19
  987.4 13.1 multiply_reduce_fusion.3
  1003.1 16.0 copy.81
  1019.0 77.6 %all_to_all.54 = bf16[2,2048,3,1,192]{4,0,3,2,1:T(2,128)(2,1)} all-to-all(bf16[2,2048,3,1,192]{4,0,3,2,1:T(2,128)(2,1)} %copy.81), channel_id=1, replica_groups=mesh['dp'=8,'head'=4] {'head'}, dimensions={1} | all-to-all | bytes 9437184 | tf_op jit(solution)/shard_map/all_to_all | solution.py:258
  1096.6 16.9 copy.97
  1164.2 32.4 %reduce-scatter.21.cloned.1.call-done = f32[192,768]{1,0:T(8,128)} async-done(((f32[768,768]{1,0:T(8,128)}), f32[192,768]{1,0:T(8,128)}) %reduce-scatter.21.cloned.1.call-update) | async-done | bytes 589840
  1198.8 34.0 %reduce-scatter.19.cloned.1.call-done = f32[192,768]{1,0:T(8,128)} async-done(((f32[768,768]{1,0:T(8,128)}), f32[192,768]{1,0:T(8,128)}) %reduce-scatter.19.cloned.1.call-update) | async-done | bytes 589840
  1235.0 34.0 %reduce-scatter.13.cloned.1.call-done = f32[192,768]{1,0:T(8,128)} async-done(((f32[768,768]{1,0:T(8,128)}), f32[192,768]{1,0:T(8,128)}) %reduce-scatter.13.cloned.1.call-update) | async-done | bytes 589840 | tf_op jit(solution)/shard_map/reduce_scatter | solution.py:277
  1269.0 81.1 %reduce-scatter.17.cloned.1.call-done = f32[768,768]{1,0:T(8,128)} async-done(((f32[3072,768]{1,0:T(8,128)}), f32[768,768]{1,0:T(8,128)}) %reduce-scatter.17.cloned.1.call-update) | async-done | bytes 2359312 | tf_op jit(solution)/shard_map/reduce_scatter | solution.py:225
  1350.1 80.9 %reduce-scatter.15.cloned.1.call-done = f32[768,768]{1,0:T(8,128)} async-done(((f32[768,3072]{1,0:T(8,128)}), f32[768,768]{1,0:T(8,128)}) %reduce-scatter.15.cloned.1.call-update) | async-done | bytes 2359312 | tf_op jit(solution)/shard_map/reduce_scatter | solution.py:224
  1472.5 39.5 %all-reduce.10 = (f32[3,3,192]{2,1,0:T(4,128)}, f32[192]{0:T(256)}, f32[192]{0:T(256)}) all-reduce(f32[3,3,192]{2,1,0:T(4,128)S(1)} %pad_maximum_fusion.1, f32[192]{0:T(256)S(1)} %dynamic-slice.15, f32[192]{0:T(256)S(1)} %dynamic-slice.17), channel_id=1, replica_groups=mesh['dp'=8,'head'=4] {'dp'}, use_global_device_ids=true, to_apply=%region_35.36 | all-reduce | flops 2112 | bytes 16896 | tf_op jit(solution)/shard_map/psum | solution.py:282
  1517.0 174.0 %all-reduce.15.cloned.1.call-done = (f32[192,768]{0,1:T(8,128)}, f32[192,768]{0,1:T(8,128)}, f32[192,768]{0,1:T(8,128)}, f32[192,768]{1,0:T(8,128)}, f32[768,768]{1,0:T(8,128)}, /*index=5*/f32[768,768]{1,0:T(8,128)}) async-done(((f32[192,768]{0,1:T(8,128)}, f32[192,768]{0,1:T(8,128)}, f32[192,768]{0,1:T(8,128)}, f32[192,768]{1,0:T(8,128)}, f32[768,768]{1,0:T(8,128)}, /*index=5*/f32[768,768]{1,0:T(8,128)}), ...) | async-done | bytes 7077904 | tf_op jit(solution)/shard_map/psum | solution.py:282
  (321 shorter events, 438.4 us)
Async XLA Ops:
  7.2 22.6 %all-gather.7.cloned.1.call-start = ((), (), s32[]{:S(2)}) async-start(), calls=%async_computation.10 | async-start | bytes 1474560 | tf_op jit(solution)/shard_map/all_gather | solution.py:168
  7.9 40.9 %all-gather.9.cloned.1.call-start = ((), (), s32[]{:S(2)}) async-start(), calls=%async_computation.11 | async-start | bytes 1474560 | tf_op jit(solution)/shard_map/all_gather | solution.py:169
  8.7 59.2 %all-gather.11.cloned.1.call-start = ((), (), s32[]{:S(2)}) async-start(), calls=%async_computation.12 | async-start | bytes 1474560 | tf_op jit(solution)/shard_map/all_gather | solution.py:170
  9.4 455.9 %all-gather.13.cloned.1.call-start = ((), (), s32[]{:S(2)}) async-start(), calls=%async_computation.13 | async-start | bytes 1474560 | tf_op jit(solution)/shard_map/all_gather | solution.py:171
  10.0 459.2 %all-gather.15.cloned.1.call-start = ((), (), s32[]{:S(2)}) async-start(), calls=%async_computation.14 | async-start | bytes 5898240 | tf_op jit(solution)/shard_map/all_gather | solution.py:205
  11.3 64.7 %copy-start.28 = (f32[768]{0:T(1024)}, f32[768]{0:T(1024)S(1)}, u32[]{:S(2)}) copy-start(f32[768]{0:T(1024)S(1)} %convert_element_type.96) | copy-start | bytes 9220
  11.7 64.3 %copy-start.30 = (f32[2,512]{1,0:T(2,128)}, f32[2,512]{1,0:T(2,128)S(1)}, u32[]{:S(2)}) copy-start(f32[2,512]{1,0:T(2,128)S(1)} %add_rsqrt_fusion.1) | copy-start | bytes 12292
  87.6 93.2 %all-to-all-start = ((bf16[2,512,3,4,192]{1,4,2,0,3:T(8,128)(2,1)}), bf16[2,512,3,4,192]{1,4,2,0,3:T(8,128)(2,1)}, u32[]{:S(2)}, u32[]{:S(2)}) async-start(bf16[2,512,3,4,192]{1,4,2,0,3:T(8,128)(2,1)} %copy.68), calls=%async_computation | async-start | bytes 9437184 | tf_op jit(solution)/shard_map/all_to_all | solution.py:178
  92.7 387.9 %all-gather.17.cloned.1.call-start = ((), (), s32[]{:S(2)}) async-start(), calls=%async_computation.15 | async-start | bytes 5898240 | tf_op jit(solution)/shard_map/all_gather | solution.py:206
  93.3 131.9 %copy-start.39 = (f32[1,1,192]{2,1,0:T(1,128)}, f32[1,1,192]{2,1,0:T(1,128)S(1)}, u32[]{:S(2)}) copy-start(f32[1,1,192]{2,1,0:T(1,128)S(1)} %get-tuple-element.309) | copy-start | bytes 2308
  93.3 131.9 %copy-start.41 = (f32[1,1,192]{2,1,0:T(1,128)}, f32[1,1,192]{2,1,0:T(1,128)S(1)}, u32[]{:S(2)}) copy-start(f32[1,1,192]{2,1,0:T(1,128)S(1)} %get-tuple-element.310) | copy-start | bytes 2308
  93.3 131.9 %copy-start.43 = (f32[1,1,192]{2,1,0:T(1,128)}, f32[1,1,192]{2,1,0:T(1,128)S(1)}, u32[]{:S(2)}) copy-start(f32[1,1,192]{2,1,0:T(1,128)S(1)} %get-tuple-element.311) | copy-start | bytes 2308
  93.4 137.6 %copy-start.33 = (f32[1,1,192]{2,1,0:T(1,128)}, f32[1,1,192]{2,1,0:T(1,128)S(1)}, u32[]{:S(2)}) copy-start(f32[1,1,192]{2,1,0:T(1,128)S(1)} %get-tuple-element.306) | copy-start | bytes 2308
  93.4 137.6 %copy-start.35 = (f32[1,1,192]{2,1,0:T(1,128)}, f32[1,1,192]{2,1,0:T(1,128)S(1)}, u32[]{:S(2)}) copy-start(f32[1,1,192]{2,1,0:T(1,128)S(1)} %get-tuple-element.307) | copy-start | bytes 2308
  93.4 137.6 %copy-start.37 = (f32[1,1,192]{2,1,0:T(1,128)}, f32[1,1,192]{2,1,0:T(1,128)S(1)}, u32[]{:S(2)}) copy-start(f32[1,1,192]{2,1,0:T(1,128)S(1)} %get-tuple-element.308) | copy-start | bytes 2308
  93.4 139.5 %copy-start.45 = (f32[1,1,192]{2,1,0:T(1,128)}, f32[1,1,192]{2,1,0:T(1,128)S(1)}, u32[]{:S(2)}) copy-start(f32[1,1,192]{2,1,0:T(1,128)S(1)} %get-tuple-element.312) | copy-start | bytes 2308
  93.4 139.5 %copy-start.47 = (f32[1,1,192]{2,1,0:T(1,128)}, f32[1,1,192]{2,1,0:T(1,128)S(1)}, u32[]{:S(2)}) copy-start(f32[1,1,192]{2,1,0:T(1,128)S(1)} %get-tuple-element.313) | copy-start | bytes 2308
  93.4 139.5 %copy-start.49 = (f32[1,1,192]{2,1,0:T(1,128)}, f32[1,1,192]{2,1,0:T(1,128)S(1)}, u32[]{:S(2)}) copy-start(f32[1,1,192]{2,1,0:T(1,128)S(1)} %get-tuple-element.314) | copy-start | bytes 2308
  254.1 12.5 copy-start.20
  298.4 12.5 copy-start.20
  342.6 12.5 copy-start.20
  386.8 12.5 copy-start.20
  428.5 29.3 %all-to-all-start.1 = ((bf16[2,2048,1,192]{3,0,2,1:T(2,128)(2,1)}), bf16[2,2048,1,192]{3,0,2,1:T(2,128)(2,1)S(1)}, u32[]{:S(2)}, u32[]{:S(2)}) async-start(bf16[2,2048,1,192]{3,0,2,1:T(2,128)(2,1)} %copy.73), calls=%async_computation.1 | async-start | bytes 4194304 | tf_op jit(solution)/shard_map/all_to_all | solution.py:197
  432.2 68.9 %copy-start.23 = (f32[768]{0:T(1024)}, f32[768]{0:T(1024)S(1)}, u32[]{:S(2)}) copy-start(f32[768]{0:T(1024)S(1)} %convert_element_type.109) | copy-start | bytes 9220
  432.3 68.8 %copy-start.51 = (pred[2,512]{1,0:T(4,128)(4,1)}, pred[2,512]{1,0:T(4,128)(4,1)S(1)}, u32[]{:S(2)}) copy-start(pred[2,512]{1,0:T(4,128)(4,1)S(1)} %broadcast_compare_fusion) | copy-start | bytes 3076
  469.2 31.9 %copy-start.12 = (f32[2,512,768]{2,1,0:T(8,128)}, f32[2,512,768]{2,1,0:T(8,128)S(1)}, u32[]{:S(2)}) copy-start(f32[2,512,768]{2,1,0:T(8,128)S(1)} %get-tuple-element.316) | copy-start | bytes 9437188
  469.2 31.9 %copy-start.25 = (f32[2,512]{1,0:T(2,128)}, f32[2,512]{1,0:T(2,128)S(1)}, u32[]{:S(2)}) copy-start(f32[2,512]{1,0:T(2,128)S(1)} %add_rsqrt_fusion) | copy-start | bytes 12292
  490.4 10.7 copy-start.13
  490.4 10.7 copy-start.19
  507.3 24.5 %all-to-all-start.2 = ((bf16[2,512,4,192]{1,3,0,2:T(8,128)(2,1)}), bf16[2,512,4,192]{1,3,0,2:T(8,128)(2,1)}, u32[]{:S(2)}, u32[]{:S(2)}) async-start(bf16[2,512,4,192]{1,3,0,2:T(8,128)(2,1)} %copy.78), calls=%async_computation.2 | async-start | bytes 3145728 | tf_op jit(solution)/shard_map/all_to_all | solution.py:236
  511.7 650.3 %reduce-scatter.23.cloned.1.call-start = ((), (), s32[]{:S(2)}) async-start(), calls=%async_computation.21 | async-start | bytes 2949120
  976.8 10.6 copy-start.4
  976.8 10.6 copy-start.6
  976.8 10.6 copy-start.34
  976.8 10.6 copy-start.36
  976.8 10.6 copy-start.38
  976.8 10.6 copy-start.40
  976.8 10.6 copy-start.42
  976.9 10.6 copy-start.44
  1127.4 69.1 %reduce-scatter.21.cloned.1.call-start = ((), (), s32[]{:S(2)}) async-start(), calls=%async_computation.20 | async-start | bytes 2949120
  1130.6 102.2 %reduce-scatter.19.cloned.1.call-start = ((), (), s32[]{:S(2)}) async-start(), calls=%async_computation.19 | async-start | bytes 2949120
  1133.7 135.3 %reduce-scatter.13.cloned.1.call-start = ((), (), s32[]{:S(2)}) async-start(), calls=%async_computation.16 | async-start | bytes 2949120 | tf_op jit(solution)/shard_map/reduce_scatter | solution.py:277
  1139.5 210.6 %reduce-scatter.17.cloned.1.call-start = ((), (), s32[]{:S(2)}) async-start(), calls=%async_computation.18 | async-start | bytes 11796480 | tf_op jit(solution)/shard_map/reduce_scatter | solution.py:225
  1150.6 280.3 %reduce-scatter.15.cloned.1.call-start = ((), (), s32[]{:S(2)}) async-start(), calls=%async_computation.17 | async-start | bytes 11796480 | tf_op jit(solution)/shard_map/reduce_scatter | solution.py:224
  1161.9 529.0 %all-reduce.15.cloned.1.call-start = ((), (), s32[]{:S(2)}) async-start(), calls=%async_computation.22 | async-start | bytes 15335424 | tf_op jit(solution)/shard_map/psum | solution.py:282
  1438.3 11.8 copy-start.8
  1438.3 11.8 copy-start.9
  1456.0 56.1 %copy-start.11 = (f32[2,512,768]{2,1,0:T(8,128)S(1)}, f32[2,512,768]{2,1,0:T(8,128)}, u32[]{:S(2)}) copy-start(f32[2,512,768]{2,1,0:T(8,128)} %copy-done.10) | copy-start | bytes 9437188
  (37 other events, 169.6 us)
Sparse Core Ops, SparseCore 0:
  9.6 20.1 all-gather.6
  31.3 17.4 all-gather.8
  50.4 17.4 all-gather.10
  69.3 17.4 all-gather.12
  88.2 62.8 all-gather.14
  152.5 46.0 all-gather.16
  1127.6 33.1 reduce-scatter.22
  1163.4 33.0 reduce-scatter.20
  1199.7 33.0 reduce-scatter.18
  1235.9 33.0 reduce-scatter.12
  1271.6 78.4 reduce-scatter.16
  1352.5 78.3 reduce-scatter.14
  1436.8 254.0 all-reduce.14
where the time goes:
time: 1720 us; the launch traced here: 1710 us
  waiting for transfers between devices  629 us (37%)
  matrix products  449 us (26%)
  local copies, waits for them, and re-layouts  242 us (14%)
  other arithmetic  219 us (13%)
  blocking collectives  123 us (7%)
    psum x1, waiting for transfers between devices, local(): lax.psum((head_query, head_key, head_value, head_out, grad_up_local, grad...  174 us
    dot_general x8, matrix products, one_block(): jnp.einsum('qhd,khd->hqk', query_rows, key_rows, preferred_element_type=j...  131 us
    all_to_all x1, waiting for transfers between devices, local(): lax.all_to_all(projected.reshape(seq_count, row_count, 3, groups, channel...  87.3 us
    convert_element_type x4, other arithmetic, one_block(): grad_low = grad_scores.astype(jnp.bfloat16)  84.6 us
    reduce_scatter x1, waiting for transfers between devices, local(): lax.psum_scatter(grad_down_part, 'head', scatter_dimension=0, tiled=True)  81.1 us
    reduce_scatter x1, waiting for transfers between devices, local(): lax.psum_scatter(grad_up_part, 'head', scatter_dimension=1, tiled=True)  80.9 us
    all_to_all x1, blocking collectives, local(): lax.all_to_all(grad_raw.reshape(seq_count, length, 3, 1, channels), 'head...  77.6 us
    dynamic_update_slice x8, local copies, waits for them, and re-layouts, attention_forward(): results, log_sums = lax.map(one_block, block_starts)  71.3 us
  transfers between devices with their start and end apart: 16, of which 12 were waited for; matrix products, arithmetic and copies ran while one was open for 21% of the time, Pallas kernels for 0%

commit v1 on v0

v1 whole, which is shorter than its diff:
```python
import functools

import jax
import jax.numpy as jnp
from jax import lax
from jax.experimental import pallas as pl
from jax.experimental.pallas import tpu as pltpu
from jax.sharding import PartitionSpec as P

HDIM = 64
EPS = 1e-06
bf16 = jnp.bfloat16
f32 = jnp.float32

NN = (((1,), (0,)), ((), ()))
NT = (((1,), (1,)), ((), ()))
TN = (((0,), (0,)), ((), ()))

CORE = [(0, 1), (1, 0), (2, 3), (3, 2)]
XNB = [(0, 2), (2, 0), (1, 3), (3, 1)]


def dot(a, b, dims=NN):
    return lax.dot_general(a, b, dims, preferred_element_type=f32)


def cost(flops, nbytes, trans=0):
    return pl.CostEstimate(flops=int(flops), bytes_accessed=int(nbytes), transcendentals=int(trans))


def sds(shape, dtype):
    return jax.ShapeDtypeStruct(shape, dtype)


def whole(shape):
    zeros = (0,) * len(shape)
    return pl.BlockSpec(shape, lambda *_: zeros, pipeline_mode=pl.Buffered(1))


def grid_spec(grid, ins, outs, scratch=()):
    return pltpu.PrefetchScalarGridSpec(
        num_scalar_prefetch=1, grid=grid, in_specs=ins, out_specs=outs, scratch_shapes=scratch
    )


def norm(x, gain):
    inv = lax.rsqrt(jnp.mean(x * x, axis=-1, keepdims=True) + EPS)
    n = x * inv
    return n, inv, (n * gain).astype(bf16)


def qkv_body(
    meta, x0, x1, x2, x3, w0, w1, w2, w3, gain, taps, h_ref, raw_ref, mix_ref, w_ref, ext
):
    b = pl.program_id(0)
    rows = x0.shape[0]
    part = w0.shape[0]

    @pl.when(b == 0)
    def _():
        for k, piece in enumerate((w0, w1, w2, w3)):
            at = jnp.bitwise_xor(meta[3], k)
            w_ref[pl.ds(pl.multiple_of(at * part, 64), part), :] = piece[...]
        ext[0:8, :] = jnp.zeros((8, ext.shape[1]), f32)

    slot = meta[4 + b]
    x = x0[...]
    for k, other in ((1, x1), (2, x2), (3, x3)):
        x = jnp.where(slot == k, other[...], x)
    _, _, h = norm(x.astype(f32), gain[...].astype(f32))
    h_ref[...] = h
    raw = dot(h, w_ref[...]).astype(bf16)
    raw_ref[...] = raw
    rawf = raw.astype(f32)
    ext[8 : 8 + rows, :] = rawf
    t = taps[...].astype(f32)
    mixed = t[0:1] * rawf + t[1:2] * ext[7 : 7 + rows, :] + t[2:3] * ext[6 : 6 + rows, :]
    mix_ref[...] = mixed.astype(bf16)
    ext[0:8, :] = ext[rows : rows + 8, :]


def qkv_call(meta, xs, ws, gain, taps):
    rows, width = xs[0].shape
    part, cols = ws[0].shape
    length = 4 * rows
    blk = lambda n: pl.BlockSpec((rows, n), lambda b, m: (b, 0))
    return pl.pallas_call(
        qkv_body,
        out_shape=[
            sds((length, width), bf16),
            sds((length, cols), bf16),
            sds((length, cols), bf16),
            sds((width, cols), bf16),
        ],
        grid_spec=grid_spec(
            (4,),
            [whole((rows, width))] * 4
            + [whole((part, cols))] * 4
            + [whole((1, width)), whole((3, cols))],
            [blk(width), blk(cols), blk(cols), pl.BlockSpec((width, cols), lambda b, m: (0, 0))],
            [pltpu.VMEM((rows + 8, cols), f32)],
        ),
        cost_estimate=cost(2 * length * width * cols, 2 * length * (width * 2 + cols * 2)),
        name="qkv",
    )(meta, *xs, *ws, gain, taps)


def two_heads(v):
    lane = lax.broadcasted_iota(jnp.int32, v.shape, 1)
    z = jnp.zeros_like(v)
    return jnp.concatenate([jnp.where(lane < HDIM, v, z), jnp.where(lane < HDIM, z, v)], axis=0)


def limits(i, rows, length):
    lim = jnp.minimum(i * rows + lax.broadcasted_iota(jnp.int32, (1, rows), 1), length - 1)
    return jnp.concatenate([lim, lim], axis=1)


def att_fwd_body(meta, q_ref, k_ref, v_ref, mine_ref, theirs_ref, lse_ref, vt, acc):
    i = pl.program_id(1)
    B = q_ref.shape[0]

    @pl.when(i == 0)
    def _():
        vt[...] = v_ref[...].T

    length = meta[0]
    qq = two_heads(q_ref[...] * bf16(HDIM**-0.5))
    acc[...] = jnp.zeros_like(acc)
    lim = limits(i, B, length)

    def tile(j, carry, masked):
        m, l = carry
        sl = pl.ds(pl.multiple_of(j * B, B), B)
        s = dot(k_ref[sl, :], qq, NT)
        if masked:
            ok = j * B + lax.broadcasted_iota(jnp.int32, (B, 2 * B), 0) <= lim
            s = jnp.where(ok, s, -1e9)
        mn = jnp.maximum(m, jnp.max(s, axis=0, keepdims=True))
        p = jnp.exp(s - mn)
        if masked:
            p = jnp.where(ok, p, 0.0)
        a = jnp.exp(m - mn)
        l = a * l + jnp.sum(p, axis=0, keepdims=True)
        pb = p.astype(bf16)
        for h in range(2):
            r, c = slice(HDIM * h, HDIM * h + HDIM), slice(h * B, h * B + B)
            acc[r, :] = acc[r, :] * a[:, c] + dot(vt[r, sl], pb[:, c])
        return mn, l

    full = jnp.minimum(i, length // B)
    init = (jnp.full((1, 2 * B), -1e9, f32), jnp.zeros((1, 2 * B), f32))
    m, l = lax.fori_loop(0, full, lambda j, c: tile(j, c, False), init)
    last = jnp.minimum(full, pl.num_programs(1) - 1)
    m, l = tile(last, (m, l), True)
    inv = 1.0 / l
    for h in range(2):
        r, c = slice(HDIM * h, HDIM * h + HDIM), slice(h * B, h * B + B)
        acc[r, :] = acc[r, :] * inv[:, c]
    out = acc[...].T.astype(bf16)
    own = jnp.bitwise_and(i, 1) == meta[2]

    @pl.when(own)
    def _():
        mine_ref[...] = out

    @pl.when(jnp.logical_not(own))
    def _():
        theirs_ref[...] = out

    ls = m + jnp.log(l)
    lse_ref[0] = jnp.concatenate([ls[:, :B], ls[:, B:]], axis=0)


def half_map(p, i, m):
    return (jnp.bitwise_xor(i // 2, m[1]), p)


def att_fwd_call(meta, mix):
    length, cols = mix.shape
    width = cols // 3
    pairs = width // 128
    B = length // 4
    half = pl.BlockSpec((B, 128), half_map)
    return pl.pallas_call(
        att_fwd_body,
        out_shape=[
            sds((length // 2, width), bf16),
            sds((length // 2, width), bf16),
            sds((pairs, 2, length), f32),
        ],
        grid_spec=grid_spec(
            (pairs, 4),
            [
                pl.BlockSpec((B, 128), lambda p, i, m: (i, p)),
                pl.BlockSpec((length, 128), lambda p, i, m: (0, pairs + p)),
                pl.BlockSpec((length, 128), lambda p, i, m: (0, 2 * pairs + p)),
            ],
            [half, half, pl.BlockSpec((1, 2, B), lambda p, i, m: (p, 0, i))],
            [pltpu.VMEM((128, length), bf16), pltpu.VMEM((128, B), f32)],
        ),
        cost_estimate=cost(8 * length * length * width, 8 * length * width, 2 * length * length * pairs),
        name="attn_fwd",
    )(meta, mix, mix, mix)


def att_bwd_body(
    meta, q_ref, k_ref, v_ref, om, ot, dm, dt, lse_ref, rq, rk, rv, taps,
    gq, gk, gv, gt, kt, dkt, dvt, dqt, dqs, ext,
):
    i = pl.program_id(1)
    B = q_ref.shape[0]
    L = k_ref.shape[0]

    @pl.when(i == 0)
    def _():
        kt[...] = k_ref[...].T
        dkt[...] = jnp.zeros_like(dkt)
        dvt[...] = jnp.zeros_like(dvt)

    length = meta[0]
    own = jnp.bitwise_and(i, 1) == meta[2]
    q = q_ref[...] * bf16(HDIM**-0.5)
    o = jnp.where(own, om[...], ot[...])
    do = jnp.where(own, dm[...], dt[...])
    qq, dd = two_heads(q), two_heads(do)
    qt, dot_ = q.T, do.T
    od = (o.astype(f32) * do.astype(f32)).T
    delta = jnp.concatenate(
        [jnp.sum(od[:HDIM], axis=0, keepdims=True), jnp.sum(od[HDIM:], axis=0, keepdims=True)],
        axis=1,
    )
    ls = lse_ref[0]
    lse = jnp.concatenate([ls[0:1], ls[1:2]], axis=1)
    dqt[...] = jnp.zeros_like(dqt)
    lim = limits(i, B, length)

    def tile(j, masked):
        sl = pl.ds(pl.multiple_of(j * B, B), B)
        s = dot(k_ref[sl, :], qq, NT)
        dp = dot(v_ref[sl, :], dd, NT)
        p = jnp.exp(s - lse)
        if masked:
            p = jnp.where(j * B + lax.broadcasted_iota(jnp.int32, (B, 2 * B), 0) <= lim, p, 0.0)
        ds = (p * (dp - delta)).astype(bf16)
        pb = p.astype(bf16)
        for h in range(2):
            r, c = slice(HDIM * h, HDIM * h + HDIM), slice(h * B, h * B + B)
            dqt[r, :] += dot(kt[r, sl], ds[:, c])
            dkt[r, sl] += dot(qt[r, :], ds[:, c], NT)
            dvt[r, sl] += dot(dot_[r, :], pb[:, c], NT)

    full = jnp.minimum(i, length // B)

    def step(j, carry):
        tile(j, False)
        return carry

    lax.fori_loop(0, full, step, 0)
    tile(jnp.minimum(full, pl.num_programs(1) - 1), True)
    dqs[pl.ds(pl.multiple_of(i * B, B), B), :] = dqt[...].T * HDIM**-0.5

    @pl.when(i == pl.num_programs(1) - 1)
    def _():
        gt[...] = jnp.zeros_like(gt)
        ext[B : B + 8, :] = jnp.zeros((8, 128), f32)
        for which, (raw, out) in enumerate(((rq, gq), (rk, gk), (rv, gv))):
            t = taps[3 * which : 3 * which + 3, :].astype(f32)
            sums = [jnp.zeros((1, 128), f32)] * 3
            for blk in reversed(range(L // B)):
                sl = slice(blk * B, blk * B + B)
                if which == 0:
                    g = dqs[sl, :]
                elif which == 1:
                    g = dkt[:, sl].T
                else:
                    g = dvt[:, sl].T
                if blk == L // B - 1:
                    ext[B : B + 8, :] = jnp.zeros((8, 128), f32)
                else:
                    ext[B : B + 8, :] = ext[0:8, :]
                ext[0:B, :] = g
                g1, g2 = ext[1 : B + 1, :], ext[2 : B + 2, :]
                out[sl, :] = (t[0:1] * g + t[1:2] * g1 + t[2:3] * g2).astype(bf16)
                r = raw[sl, :].astype(f32)
                for n, gg in enumerate((g, g1, g2)):
                    sums[n] = sums[n] + jnp.sum(r * gg, axis=0, keepdims=True)
            for n in range(3):
                gt[3 * which + n : 3 * which + n + 1, :] = sums[n]


def att_bwd_call(meta, mix, raw, om, ot, dm, dt, lse, taps):
    length, cols = mix.shape
    width = cols // 3
    pairs = width // 128
    B = length // 4
    half = pl.BlockSpec((B, 128), half_map)
    full = lambda k: pl.BlockSpec((length, 128), lambda p, i, m: (0, k * pairs + p))
    return pl.pallas_call(
        att_bwd_body,
        out_shape=[sds((length, width), bf16)] * 3 + [sds((16, width), f32)],
        grid_spec=grid_spec(
            (pairs, 4),
            [
                pl.BlockSpec((B, 128), lambda p, i, m: (i, p)),
                full(1),
                full(2),
                half,
                half,
                half,
                half,
                pl.BlockSpec((1, 2, B), lambda p, i, m: (p, 0, i)),
                full(0),
                full(1),
                full(2),
                pl.BlockSpec((9, 128), lambda p, i, m: (0, p)),
            ],
            [full(0)] * 3 + [pl.BlockSpec((16, 128), lambda p, i, m: (0, p))],
            [
                pltpu.VMEM((128, length), bf16),
                pltpu.VMEM((128, length), f32),
                pltpu.VMEM((128, length), f32),
                pltpu.VMEM((128, B), f32),
                pltpu.VMEM((length, 128), f32),
                pltpu.VMEM((B + 8, 128), f32),
            ],
        ),
        cost_estimate=cost(14 * length * length * width, 20 * length * width, 2 * length * length * pairs),
        name="attn_bwd",
    )(meta, mix, mix, mix, om, ot, dm, dt, lse, raw, raw, raw, taps)


T = 256


def row_valid(meta, i, per):
    block = jnp.where(i < per, meta[3], jnp.bitwise_xor(meta[3], 2))
    start = block * (per * T) + lax.rem(i, per) * T
    return start + lax.broadcasted_iota(jnp.int32, (T, 1), 0) < meta[0]


def mid_body(meta, xo, xx, co, cx, am, at, w, gain, mid_ref, h_ref, g_ref):
    i = pl.program_id(0)
    per = pl.num_programs(0) // 2
    first = i < per
    x = jnp.where(first, xo[...], xx[...]).astype(f32)
    mid = x + dot(jnp.concatenate([am[...], at[...]], axis=1), w[...])
    mid_ref[...] = mid
    h_ref[...] = norm(mid, gain[...].astype(f32))[2]
    ct = jnp.where(first, co[...], cx[...])
    g_ref[...] = jnp.where(row_valid(meta, i, per), ct, jnp.zeros_like(ct))


def own_map(per):
    return lambda i, m: (jnp.minimum(i, per - 1), 0)


def nb_map(per):
    return lambda i, m: (jnp.maximum(i - per, 0), 0)


def mid_call(meta, xo, xx, co, cx, am, at, w, gain):
    rows, width = xo.shape
    per = rows // T
    half = am.shape[1]
    fst, snd = pl.BlockSpec((T, width), own_map(per)), pl.BlockSpec((T, width), nb_map(per))
    blk = lambda n: pl.BlockSpec((T, n), lambda i, m: (i, 0))
    return pl.pallas_call(
        mid_body,
        out_shape=[
            sds((2 * rows, width), f32),
            sds((2 * rows, width), bf16),
            sds((2 * rows, width), bf16),
        ],
        grid_spec=grid_spec(
            (2 * per,),
            [fst, snd, fst, snd, blk(half), blk(half), whole((width, width)), whole((1, width))],
            [blk(width)] * 3,
        ),
        cost_estimate=cost(4 * rows * width * width, 24 * rows * width),
        name="mid",
    )(meta, xo, xx, co, cx, am, at, w, gain)


def ff_body(first, meta, h_ref, g_ref, wu, wd, *rest):
    if first:
        fo, dh, gu, gd, au, ad = rest
    else:
        fi, di, fo, dh, gu, gd, au, ad = rest
    i = pl.program_id(0)
    h, g = h_ref[...], g_ref[...]
    u = dot(h, wu[...])
    r = jnp.maximum(u, 0.0)
    act = (r * r).astype(bf16)
    du = (dot(g, wd[...], NT) * 2.0 * r).astype(bf16)
    f = dot(act, wd[...])
    d = dot(du, wu[...], NT)
    fo[...] = f if first else fi[...] + f
    dh[...] = d if first else di[...] + d
    pu = dot(h, du, TN)
    pd = dot(act, g, TN)

    @pl.when(i == 0)
    def _():
        au[...] = pu
        ad[...] = pd

    @pl.when(i > 0)
    def _():
        au[...] += pu
        ad[...] += pd

    @pl.when(i == pl.num_programs(0) - 1)
    def _():
        gu[...] = au[...].astype(bf16)
        gd[...] = ad[...].astype(bf16)


def ff_call(meta, h, g, wu, wd, carry):
    rows, width = h.shape
    hid = wu.shape[1]
    blk = pl.BlockSpec((T, width), lambda i, m: (i, 0))
    const = lambda s: pl.BlockSpec(s, lambda i, m: (0, 0), pipeline_mode=pl.Buffered(1))
    first = carry is None
    extra = () if first else carry
    return pl.pallas_call(
        functools.partial(ff_body, first),
        out_shape=[
            sds((rows, width), f32),
            sds((rows, width), f32),
            sds((width, hid), bf16),
            sds((hid, width), bf16),
        ],
        grid_spec=grid_spec(
            (rows // T,),
            [blk, blk, const((width, hid)), const((hid, width))] + [blk] * len(extra),
            [blk, blk, const((width, hid)), const((hid, width))],
            [pltpu.VMEM((width, hid), f32), pltpu.VMEM((hid, width), f32)],
        ),
        cost_estimate=cost(12 * rows * width * hid, 20 * rows * width + 8 * width * hid),
        name="ff",
    )(meta, h, g, wu, wd, *extra)


def epi_body(
    meta, mid_ref, f_ref, dh_ref, co, cx, am, at, w, gain,
    oo, ox, dmid_ref, dm_ref, dt_ref, gm, gt, gg, acc,
):
    i = pl.program_id(0)
    per = pl.num_programs(0) // 2
    first = i < per
    ok = row_valid(meta, i, per)
    mid = mid_ref[...]
    out = jnp.where(ok, mid + f_ref[...], 0.0)

    @pl.when(first)
    def _():
        oo[...] = out

    @pl.when(jnp.logical_not(first))
    def _():
        ox[...] = out.astype(bf16)

    g = jnp.where(ok, jnp.where(first, co[...], cx[...]).astype(f32), 0.0)
    gn = gain[...].astype(f32)
    n, inv, _ = norm(mid, gn)
    dh = dh_ref[...]
    dn = dh * gn
    dmid = g + inv * (dn - n * jnp.mean(dn * n, axis=-1, keepdims=True))
    dmid_ref[...] = dmid
    db = dmid.astype(bf16)
    half = am.shape[1]
    da = dot(db, w[...], NT).astype(bf16)
    dm_ref[...] = da[:, :half]
    dt_ref[...] = da[:, half:]
    a = jnp.concatenate([am[...], at[...]], axis=1)
    pg = dot(a, db, TN)
    ps = jnp.sum(dh * n, axis=0, keepdims=True)

    @pl.when(i == 0)
    def _():
        acc[...] = pg
        gg[...] = ps

    @pl.when(i > 0)
    def _():
        acc[...] += pg
        gg[...] += ps

    @pl.when(i == pl.num_programs(0) - 1)
    def _():
        gm[...] = acc[0:half, :].astype(bf16)
        gt[...] = acc[half:, :].astype(bf16)


def epi_call(meta, mid, f, dh, co, cx, am, at, w, gain):
    rows, width = co.shape
    per = rows // T
    half = am.shape[1]
    fst, snd = pl.BlockSpec((T, width), own_map(per)), pl.BlockSpec((T, width), nb_map(per))
    blk = lambda n: pl.BlockSpec((T, n), lambda i, m: (i, 0))
    const = lambda s: pl.BlockSpec(s, lambda i, m: (0, 0), pipeline_mode=pl.Buffered(1))
    return pl.pallas_call(
        epi_body,
        out_shape=[
            sds((rows, width), f32),
            sds((rows, width), bf16),
            sds((2 * rows, width), f32),
            sds((2 * rows, half), bf16),
            sds((2 * rows, half), bf16),
            sds((half, width), bf16),
            sds((half, width), bf16),
            sds((1, width), f32),
        ],
        grid_spec=grid_spec(
            (2 * per,),
            [blk(width)] * 3
            + [fst, snd, blk(half), blk(half), whole((width, width)), whole((1, width))],
            [
                fst,
                snd,
                blk(width),
                blk(half),
                blk(half),
                const((half, width)),
                const((half, width)),
                const((1, width)),
            ],
            [pltpu.VMEM((width, width), f32)],
        ),
        cost_estimate=cost(8 * rows * width * width, 50 * rows * width),
        name="epi",
    )(meta, mid, f, dh, co, cx, am, at, w, gain)


def proj_body(meta, h_ref, q, k, v, w, dm, dt, keep, send, acc):
    b = pl.program_id(0)
    d = jnp.concatenate([q[...], k[...], v[...]], axis=1)
    dh = dot(d, w[...], NT)
    own = jnp.bitwise_and(b, 1) == meta[2]

    @pl.when(own)
    def _():
        dm[...] = dh

    @pl.when(jnp.logical_not(own))
    def _():
        dt[...] = dh.astype(bf16)

    pg = dot(h_ref[...], d, TN)

    @pl.when(b == 0)
    def _():
        acc[...] = pg

    @pl.when(b > 0)
    def _():
        acc[...] += pg

    @pl.when(b == pl.num_programs(0) - 1)
    def _():
        part = keep.shape[1]
        for ref, n, k_ in ((keep, 0, 0), (keep, 1, 2), (send, 0, 1), (send, 1, 3)):
            at = jnp.bitwise_xor(meta[3], k_)
            ref[n] = acc[pl.ds(pl.multiple_of(at * part, 64), part), :].astype(bf16)


def proj_call(meta, h, q, k, v, w):
    length, width = h.shape
    half = q.shape[1]
    B = length // 4
    part = width // 4
    blk = lambda n: pl.BlockSpec((B, n), lambda b, m: (b, 0))
    side = pl.BlockSpec((B, width), lambda b, m: (jnp.bitwise_xor(b // 2, m[1]), 0))
    g = pl.BlockSpec((2, part, 3 * half), lambda b, m: (0, 0, 0), pipeline_mode=pl.Buffered(1))
    return pl.pallas_call(
        proj_body,
        out_shape=[
            sds((length // 2, width), f32),
            sds((length // 2, width), bf16),
            sds((2, part, 3 * half), bf16),
            sds((2, part, 3 * half), bf16),
        ],
        grid_spec=grid_spec(
            (4,),
            [blk(width), blk(half), blk(half), blk(half), whole((width, 3 * half))],
            [side, side, g, g],
            [pltpu.VMEM((width, 3 * half), f32)],
        ),
        cost_estimate=cost(12 * length * width * half, 12 * length * width),
        name="proj",
    )(meta, h, q, k, v, w)


def last_body(meta, xo, xx, dm, dt, dmid, gain, go, gx, gg):
    i = pl.program_id(0)
    per = pl.num_programs(0) // 2
    first = i < per
    x = jnp.where(first, xo[...], xx[...]).astype(f32)
    gn = gain[...].astype(f32)
    n, inv, _ = norm(x, gn)
    dh = dm[...] + dt[...].astype(f32)
    dn = dh * gn
    out = dmid[...] + inv * (dn - n * jnp.mean(dn * n, axis=-1, keepdims=True))

    @pl.when(first)
    def _():
        go[...] = out

    @pl.when(jnp.logical_not(first))
    def _():
        gx[...] = out.astype(bf16)

    ps = jnp.sum(dh * n, axis=0, keepdims=True)

    @pl.when(i == 0)
    def _():
        gg[...] = ps

    @pl.when(i > 0)
    def _():
        gg[...] += ps


def last_call(meta, xo, xx, dm, dt, dmid, gain):
    rows, width = xo.shape
    per = rows // T
    fst, snd = pl.BlockSpec((T, width), own_map(per)), pl.BlockSpec((T, width), nb_map(per))
    blk = pl.BlockSpec((T, width), lambda i, m: (i, 0))
    return pl.pallas_call(
        last_body,
        out_shape=[sds((rows, width), f32), sds((rows, width), bf16), sds((1, width), f32)],
        grid_spec=grid_spec(
            (2 * per,),
            [fst, snd, blk, blk, blk, whole((1, width))],
            [fst, snd, pl.BlockSpec((1, width), lambda i, m: (0, 0))],
        ),
        cost_estimate=cost(40 * rows * width, 30 * rows * width),
        name="last",
    )(meta, xo, xx, dm, dt, dmid, gain)


def flip(size, bit):
    return [(i, i ^ bit) for i in range(size)]


def reduce_dp(v, size):
    me = lax.axis_index("dp")
    bits = []
    bit = 1
    while bit < size:
        bits.append(bit)
        bit *= 2
    for bit in bits:
        half = v.shape[0] // 2
        mine = jnp.where(jnp.bitwise_and(me, bit) > 0, 1, 0)
        send = lax.dynamic_slice_in_dim(v, (1 - mine) * half, half, 0).astype(bf16)
        got = lax.ppermute(send, "dp", flip(size, bit))
        v = lax.dynamic_slice_in_dim(v, mine * half, half, 0) + got.astype(f32)
    v = v.astype(bf16)
    for bit in reversed(bits):
        got = lax.ppermute(v, "dp", flip(size, bit))
        upper = jnp.bitwise_and(me, bit) > 0
        v = jnp.where(upper, jnp.concatenate([got, v], 0), jnp.concatenate([v, got], 0))
    return v


def sum_small(v, size):
    bit = 1
    while bit < size:
        v = v + lax.ppermute(v, "dp", flip(size, bit))
        bit *= 2
    return v


def core_swap(v):
    return lax.ppermute(v, "head", CORE)


def x_swap(v):
    return lax.ppermute(v, "head", XNB)


def local(dp, inputs, lengths, w_query, w_key, w_value, w_out, w_up, w_down, conv_taps, gain_attn, gain_ff, cotangent):
    hd = lax.axis_index("head")
    x, c = hd // 2, hd % 2
    width = inputs.shape[2]
    part = w_query.shape[0]
    pick = lambda v, k: lax.dynamic_index_in_dim(v, k, 0, keepdims=False)
    first = x == 0
    order = lambda own, nb: jnp.where(first, jnp.stack([own, nb]), jnp.stack([nb, own]))

    slots = [jnp.bitwise_xor(hd, b) for b in range(4)]
    slots = [jnp.bitwise_and(s, 1) * 2 + s // 2 for s in slots]
    meta = jnp.stack([pick(lengths, x), x, c, hd, *slots]).astype(jnp.int32)

    x_own, x_nb = pick(inputs, x), x_swap(pick(inputs, 1 - x))
    w3 = jnp.stack([w_query, w_key, w_value], axis=1).reshape(part, 3, 4, part)
    even = w3[:, :, 0::2].reshape(part, -1)
    odd = w3[:, :, 1::2].reshape(part, -1)
    w_mine = jnp.where(c == 0, even, odd)
    w_core = core_swap(jnp.where(c == 0, odd, even))
    w_pair = x_swap(jnp.stack([w_mine, w_core]))
    x_core, x_cnb = core_swap(x_own), core_swap(x_nb)
    taps_nb = x_swap(conv_taps)
    taps = order(conv_taps, taps_nb)
    taps9 = taps.transpose(1, 2, 0, 3).reshape(9, 2 * part)
    taps3 = taps.transpose(2, 1, 0, 3).reshape(3, 6 * part)
    gain1, gain2 = gain_attn.reshape(1, width), gain_ff.reshape(1, width)
    h1, raw, mix, w_full = qkv_call(
        meta, (x_own, x_nb, x_core, x_cnb), (w_mine, w_core, w_pair[0], w_pair[1]), gain1, taps3
    )
    wo_nb = x_swap(w_out)
    wo_mine = order(w_out, wo_nb).reshape(2 * part, width)
    wo = jnp.concatenate([wo_mine, core_swap(wo_mine)], axis=0)
    c_own, c_nb = pick(cotangent, x), x_swap(pick(cotangent, 1 - x))
    up_nb, down_nb = x_swap(w_up), x_swap(w_down)
    up_core, down_core = core_swap(w_up), core_swap(w_down)
    up_cnb, down_cnb = core_swap(up_nb), core_swap(down_nb)

    a_mine, a_send, lse = att_fwd_call(meta, mix)
    a_got = core_swap(a_send)
    mid, h2, g = mid_call(meta, x_own, x_nb, c_own, c_nb, a_mine, a_got, wo, gain2)
    f, dh, gu_c, gd_c = ff_call(meta, h2, g, up_core, down_core, None)
    f, dh, gu_cn, gd_cn = ff_call(meta, h2, g, up_cnb, down_cnb, (f, dh))
    f, dh, gu_n, gd_n = ff_call(meta, h2, g, up_nb, down_nb, (f, dh))
    f, dh, gu_o, gd_o = ff_call(meta, h2, g, w_up, w_down, (f, dh))
    out_own, out_nb, dmid, d_mine, d_send, go_mine, go_send, gg2 = epi_call(
        meta, mid, f, dh, c_own, c_nb, a_mine, a_got, wo, gain2
    )
    d_got = core_swap(d_send)

    both = lambda a, b: a.astype(f32) + b.astype(f32)
    gu_n = both(gu_n, core_swap(gu_cn))
    gd_n = both(gd_n, core_swap(gd_cn))
    gu_o = both(gu_o, core_swap(gu_c))
    gd_o = both(gd_o, core_swap(gd_c))
    gu_o = gu_o + x_swap(gu_n.astype(bf16)).astype(f32)
    gd_o = gd_o + x_swap(gd_n.astype(bf16)).astype(f32)
    go = both(go_mine, core_swap(go_send)).reshape(2, part, width)
    go_o = pick(go, x) + x_swap(pick(go, 1 - x).astype(bf16)).astype(f32)
    grad_up = reduce_dp(gu_o, dp).astype(f32)
    grad_down = reduce_dp(gd_o, dp).astype(f32)
    grad_out = reduce_dp(go_o, dp).astype(f32)
    output = order(out_own, x_swap(out_nb).astype(f32))

    dq, dk, dv, gt = att_bwd_call(meta, mix, raw, a_mine, a_send, d_mine, d_got, lse, taps9)
    dh_mine, dh_send, gp_keep, gp_send = proj_call(meta, h1, dq, dk, dv, w_full)
    gp_got = core_swap(gp_send)
    dh_got = core_swap(dh_send)
    gp = jnp.concatenate([gp_keep, gp_got], axis=2)
    gp_sum = gp[0].astype(f32) + x_swap(gp[1]).astype(f32)
    gp_all = reduce_dp(gp_sum, dp)
    gi_own, gi_nb, gg1 = last_call(meta, x_own, x_nb, dh_mine, dh_got, dmid, gain1)
    grad_input = order(gi_own, x_swap(gi_nb).astype(f32))

    gains = jnp.concatenate([gg1, gg2], axis=0)
    gains = gains + core_swap(gains)
    gains = gains + x_swap(gains)
    gt = gt[:9].reshape(9, 2, part).transpose(1, 0, 2)
    gt = pick(gt, x) + x_swap(pick(gt, 1 - x))
    gains = lax.dynamic_slice_in_dim(gains, hd * part, part, 1)
    small = sum_small(jnp.concatenate([gt, gains], axis=0), dp)
    grad_taps = small[:9].reshape(3, 3, part)

    gp_all = gp_all.astype(f32).reshape(part, 2, 3, 2, part)
    mine, other = gp_all[:, 0], gp_all[:, 1]
    lo = jnp.where(c == 0, mine, other)
    hi = jnp.where(c == 0, other, mine)
    full = jnp.stack([lo, hi], axis=3).reshape(part, 3, width)
    return (
        output,
        grad_input,
        full[:, 0],
        full[:, 1],
        full[:, 2],
        grad_out,
        grad_up,
        grad_down,
        grad_taps,
        small[9],
        small[10],
    )


def solution(mesh):
    placed = (
        P("dp", "head", None),
        P("dp"),
        P("head", None),
        P("head", None),
        P("head", None),
        P("head", None),
        P(None, "head"),
        P("head", None),
        P(None, None, "head"),
        P(),
        P(),
        P("dp", "head", None),
    )
    return jax.shard_map(
        functools.partial(local, mesh.shape["dp"]),
        mesh=mesh,
        in_specs=placed,
        out_specs=(
            P("dp", "head", None),
            P("dp", "head", None),
            P("head", None),
            P("head", None),
            P("head", None),
            P("head", None),
            P(None, "head"),
            P("head", None),
            P(None, None, "head"),
            P("head"),
            P("head"),
        ),
        check_vma=False,
    )
```

time: 1720 us -> 584 us (0.34)
  matrix products: 449 us -> 0 us
  waiting for transfers between devices: 629 us -> 202 us
  Pallas kernels: 0 us -> 218 us
  local copies, waits for them, and re-layouts: 242 us -> 44.6 us
  other arithmetic: 219 us -> 44.2 us
  blocking collectives: 123 us -> 0 us
  starting transfers between devices: 13.8 us -> 62.3 us
    dot_general x40 -> x0, matrix products: 449 us -> none  [the longest x8 131 us: one_block(): jnp.einsum('qhd,khd->hqk', query_rows, key_rows, preferred_element_type=j...]
    pallas_call x0 -> x11, Pallas kernels: none -> 218 us  [the longest x1 61.5 us: att_bwd_call(): pl.pallas_call(att_bwd_body, out_shape=[sds((length, width), bf16)] * 3 +...]
    ppermute x0 -> x60, waiting for transfers between devices: none -> 202 us  [the longest x15 133 us: x_swap(): return lax.ppermute(v, 'head', XNB)]
    reduce_scatter x3 -> x0, waiting for transfers between devices: 196 us -> none  [the longest x1 81.1 us: local(): lax.psum_scatter(grad_down_part, 'head', scatter_dimension=0, tiled=True)]
    psum x1 -> x0, waiting for transfers between devices: 174 us -> none  [local(): lax.psum((head_query, head_key, head_value, head_out, grad_up_local, grad...]
    all_to_all x3 -> x0, waiting for transfers between devices: 133 us -> none  [the longest x1 87.3 us: local(): lax.all_to_all(projected.reshape(seq_count, row_count, 3, groups, channel...]
    convert_element_type x10, other arithmetic: 103 us -> 15.2 us  [the longest x1 3.03 us: local(): gu_o = gu_o + x_swap(gu_n.astype(bf16)).astype(f32)]
    reduce_sum x12 -> x0, other arithmetic: 79.4 us -> none  [the longest x4 49.8 us: one_block(): row_total = jnp.sum(raised, axis=-1, keepdims=True)]
  transfers between devices with their start and end apart: 16 -> 60, of which waited for: 12 -> 29; matrix products, arithmetic and copies ran while one was open for 21% -> 11% of each run, Pallas kernels for 0% -> 28%
where the time goes in v1:
time: 584 us; the launch traced here: 573 us
  Pallas kernels  218 us (37%)
  waiting for transfers between devices  202 us (35%)
  starting transfers between devices  62.3 us (11%)
  local copies, waits for them, and re-layouts  44.6 us (8%)
  other arithmetic  44.2 us (8%)
    ppermute x15, waiting for transfers between devices, x_swap(): return lax.ppermute(v, 'head', XNB)  133 us
    pallas_call x1, Pallas kernels, att_bwd_call(): pl.pallas_call(att_bwd_body, out_shape=[sds((length, width), bf16)] * 3 +...  61.5 us
    pallas_call x4, Pallas kernels, ff_call(): pl.pallas_call(functools.partial(ff_body, first), out_shape=[sds((rows, w...  61 us
    ppermute x12, waiting for transfers between devices, reduce_dp(): got = lax.ppermute(send, 'dp', flip(size, bit))  42.5 us
    pallas_call x1, Pallas kernels, att_fwd_call(): pl.pallas_call(att_fwd_body, out_shape=[sds((length // 2, width), bf16),...  38 us
    ppermute x12, waiting for transfers between devices, reduce_dp(): got = lax.ppermute(v, 'dp', flip(size, bit))  24.5 us
    ppermute x12, starting transfers between devices, reduce_dp(): got = lax.ppermute(send, 'dp', flip(size, bit))  19.4 us
    pallas_call x1, Pallas kernels, proj_call(): pl.pallas_call(proj_body, out_shape=[sds((length // 2, width), f32), sds(...  18.3 us
  transfers between devices with their start and end apart: 60, of which 29 were waited for; matrix products, arithmetic and copies ran while one was open for 11% of the time, Pallas kernels for 28%

profile of v1, /device:TPU:0, one launch (start us, length us, event | category | flops | bytes accessed | tf_op | source)
XLA Modules:
  0.0 572.8 jit_solution(7106093837894840259)
XLA Ops:
  4.7 5.1 slice.46
  9.8 5.1 slice.45
  17.4 2.4 dynamic-slice_bitcast_fusion.2
  19.8 2.5 collective-permute-start
  25.8 15.0 %collective-permute-done.x1.xx = bf16[512,768]{1,0:T(8,128)(2,1)S(1)} collective-permute-done((bf16[512,768]{1,0:T(8,128)(2,1)}, bf16[512,768]{1,0:T(8,128)(2,1)S(1)}, u32[]{:S(2)}, u32[]{:S(2)}) %collective-permute-start) | collective-permute-done | bytes 786464 | tf_op jit(solution)/shard_map/ppermute | solution.py:681
  45.9 20.2 %collective-permute-done.6 = bf16[3,3,192]{2,1,0:T(4,128)(2,1)S(1)} collective-permute-done((bf16[3,3,192]{2,1,0:T(4,128)(2,1)S(1)}, bf16[3,3,192]{2,1,0:T(4,128)(2,1)S(1)}, u32[]{:S(2)}, u32[]{:S(2)}) %collective-permute-start.6) | collective-permute-done | bytes 3488 | tf_op jit(solution)/shard_map/ppermute | solution.py:681
  75.1 12.1 %qkv.1 = (bf16[2048,768]{1,0:T(8,128)(2,1)}, bf16[2048,1152]{1,0:T(8,128)(2,1)}, bf16[2048,1152]{1,0:T(8,128)(2,1)}, bf16[768,1152]{1,0:T(8,128)(2,1)}) custom-call(s32[8]{0:T(128)} %stack.118.meta, bf16[512,768]{1,0:T(8,128)(2,1)} %copy-done.2, bf16[512,768]{1,0:T(8,128)(2,1)} %copy-done.4, bf16[512,768]{1,0:T(8,128)(2,1)} %collective-permute-done.2.x2, ...), custom_call_target="tpu_custom_call" | custom-call | flops 3623878656 | bytes 15728640 | tf_op jit(solution)/shard_map/qkv/pallas_call | solution.py:87
  87.2 24.8 %collective-permute-done.1.cx = bf16[512,768]{1,0:T(8,128)(2,1)S(1)} collective-permute-done((bf16[512,768]{1,0:T(8,128)(2,1)}, bf16[512,768]{1,0:T(8,128)(2,1)S(1)}, u32[]{:S(2)}, u32[]{:S(2)}) %collective-permute-start.1) | collective-permute-done | bytes 786464 | tf_op jit(solution)/shard_map/ppermute | solution.py:681
  112.0 38.0 %attn_fwd.1 = (bf16[1024,384]{1,0:T(8,128)(2,1)}, bf16[1024,384]{1,0:T(8,128)(2,1)}, f32[3,2,2048]{2,1,0:T(2,128)}) custom-call(s32[8]{0:T(128)} %stack.118.meta, bf16[2048,1152]{1,0:T(8,128)(2,1)} %get-tuple-element.56.q_ref.k_ref.v_ref, bf16[2048,1152]{1,0:T(8,128)(2,1)} %get-tuple-element.56.q_ref.k_ref.v_ref, ...), custom_call_target="tpu_custom_call" | custom-call | flops 12884901888 | bytes 6291456 | tf_op jit(solution)/shard_map/attn_fwd/pallas_call | solution.py:185
  153.9 7.2 %mid.1 = (f32[1024,768]{1,0:T(8,128)}, bf16[1024,768]{1,0:T(8,128)(2,1)}, bf16[1024,768]{1,0:T(8,128)(2,1)}) custom-call(s32[8]{0:T(128)} %stack.118.meta, bf16[512,768]{1,0:T(8,128)(2,1)} %copy-done.2, bf16[512,768]{1,0:T(8,128)(2,1)} %copy-done.4, bf16[512,768]{1,0:T(8,128)(2,1)} %get-tuple-element.105.co, bf16[512,768]{1,0:T(8,128)(2,1)} %copy-done.5, ...), custom_call_target="tpu_custom_call" | custom-call | flops 1207959552 | bytes 9437184 | tf_op jit(solution)/shard_map/mid/pallas_call | solution.py:368
  161.1 15.1 %ff.4 = (f32[1024,768]{1,0:T(8,128)}, f32[1024,768]{1,0:T(8,128)}, bf16[768,768]{1,0:T(8,128)(2,1)}, bf16[768,768]{1,0:T(8,128)(2,1)}) custom-call(s32[8]{0:T(128)} %stack.118.meta, bf16[1024,768]{1,0:T(8,128)(2,1)} %get-tuple-element.60.h_ref, bf16[1024,768]{1,0:T(8,128)(2,1)} %get-tuple-element.61.g_ref, bf16[768,768]{1,0:T(8,128)(2,1)} %collective-permute-done.14.wu, ...), custom_call_target="tpu_custom_call" | custom-call | flops 7247757312 | bytes 20447232 | tf_op jit(solution)/shard_map/ff/pallas_call | solution.py:426
  176.2 15.3 %ff.5 = (f32[1024,768]{1,0:T(8,128)}, f32[1024,768]{1,0:T(8,128)}, bf16[768,768]{1,0:T(8,128)(2,1)}, bf16[768,768]{1,0:T(8,128)(2,1)}) custom-call(s32[8]{0:T(128)} %stack.118.meta, bf16[1024,768]{1,0:T(8,128)(2,1)} %get-tuple-element.60.h_ref, bf16[1024,768]{1,0:T(8,128)(2,1)} %get-tuple-element.61.g_ref, bf16[768,768]{1,0:T(8,128)(2,1)} %collective-permute-done.12.wu, ...), custom_call_target="tpu_custom_call" | custom-call | flops 7247757312 | bytes 20447232 | tf_op jit(solution)/shard_map/ff/pallas_call | solution.py:426
  191.5 15.3 %ff.6 = (f32[1024,768]{1,0:T(8,128)}, f32[1024,768]{1,0:T(8,128)}, bf16[768,768]{1,0:T(8,128)(2,1)}, bf16[768,768]{1,0:T(8,128)(2,1)}) custom-call(s32[8]{0:T(128)} %stack.118.meta, bf16[1024,768]{1,0:T(8,128)(2,1)} %get-tuple-element.60.h_ref, bf16[1024,768]{1,0:T(8,128)(2,1)} %get-tuple-element.61.g_ref, bf16[768,768]{1,0:T(8,128)(2,1)} %collective-permute-done.10.wu, ...), custom_call_target="tpu_custom_call" | custom-call | flops 7247757312 | bytes 20447232 | tf_op jit(solution)/shard_map/ff/pallas_call | solution.py:426
  206.9 15.3 %ff.7 = (f32[1024,768]{1,0:T(8,128)}, f32[1024,768]{1,0:T(8,128)}, bf16[768,768]{1,0:T(8,128)(2,1)}, bf16[768,768]{1,0:T(8,128)(2,1)}) custom-call(s32[8]{0:T(128)} %stack.118.meta, bf16[1024,768]{1,0:T(8,128)(2,1)} %get-tuple-element.60.h_ref, bf16[1024,768]{1,0:T(8,128)(2,1)} %get-tuple-element.61.g_ref, bf16[768,768]{1,0:T(8,128)(2,1)} %wu.1, ...), custom_call_target="tpu_custom_call" | custom-call | flops 7247757312 | bytes 20447232 | tf_op jit(solution)/shard_map/ff/pallas_call | solution.py:426
  222.2 12.6 %epi.1 = (f32[512,768]{1,0:T(8,128)}, bf16[512,768]{1,0:T(8,128)(2,1)}, f32[1024,768]{1,0:T(8,128)}, bf16[1024,384]{1,0:T(8,128)(2,1)}, bf16[1024,384]{1,0:T(8,1...) custom-call(s32[8]{0:T(128)} %stack.118.meta, ...), custom_call_target="tpu_custom_call" | custom-call | flops 2415919104 | bytes 19660800 | tf_op jit(solution)/shard_map/epi/pallas_call | solution.py:503
  241.3 61.5 %attn_bwd.1 = (bf16[2048,384]{1,0:T(8,128)(2,1)}, bf16[2048,384]{1,0:T(8,128)(2,1)}, bf16[2048,384]{1,0:T(8,128)(2,1)}, f32[16,384]{1,0:T(8,128)}) custom-call(s32[8]{0:T(128)} %stack.118.meta, bf16[2048,1152]{1,0:T(8,128)(2,1)} %get-tuple-element.56.q_ref.k_ref.v_ref, bf16[2048,1152]{1,0:T(8,128)(2,1)} %get-tuple-element.56.q_ref.k_ref.v_ref, ...), custom_call_target="tpu_custom_call" | custom-call | flops 22548578304 | bytes 15728640 | tf_op jit(solution)/shard_map/attn_bwd/pallas_call | solution.py:299
  302.8 18.3 %proj.1 = (f32[1024,768]{1,0:T(8,128)}, bf16[1024,768]{1,0:T(8,128)(2,1)}, bf16[2,192,1152]{2,1,0:T(8,128)(2,1)}, bf16[2,192,1152]{2,1,0:T(8,128)(2,1)}) custom-call(s32[8]{0:T(128)} %stack.118.meta, bf16[2048,768]{1,0:T(8,128)(2,1)} %get-tuple-element.72.h_ref, bf16[2048,384]{1,0:T(8,128)(2,1)} %get-tuple-element.77.q, ...), custom_call_target="tpu_custom_call" | custom-call | flops 7247757312 | bytes 18874368 | tf_op jit(solution)/shard_map/proj/pallas_call | solution.py:576
  323.0 5.7 %collective-permute-done.30 = bf16[96,768]{1,0:T(8,128)(2,1)S(1)} collective-permute-done((bf16[96,768]{1,0:T(8,128)(2,1)S(1)}, bf16[96,768]{1,0:T(8,128)(2,1)S(1)}, u32[]{:S(2)}, u32[]{:S(2)}) %collective-permute-start.30) | collective-permute-done | bytes 147488 | tf_op jit(solution)/shard_map/ppermute | solution.py:658
  334.8 2.6 collective-permute-start.32
  337.5 2.2 collective-permute-done.32
  340.9 2.6 collective-permute-done.54
  343.5 2.7 collective-permute-start.33
  350.0 3.0 add_convert_fusion.1
  354.3 2.6 add_convert_fusion
  356.9 2.6 collective-permute-done.35
  363.7 7.3 %last.1 = (f32[512,768]{1,0:T(8,128)}, bf16[512,768]{1,0:T(8,128)(2,1)}, f32[1,768]{1,0:T(1,128)}) custom-call(s32[8]{0:T(128)} %stack.118.meta, bf16[512,768]{1,0:T(8,128)(2,1)} %copy-done.2, bf16[512,768]{1,0:T(8,128)(2,1)} %copy-done.4, f32[1024,768]{1,0:T(8,128)} %get-tuple-element.81.dm, bf16[1024,768]{1,0:T(8,128)(2,1)} %copy-done.10, ...), custom_call_target="tpu_custom_call" | custom-call | flops 15728640 | bytes 11796480 | tf_op jit(solution)/shard_map/last/pallas_call | solution.py:630
  375.2 13.5 %collective-permute-done.38 = bf16[768,768]{1,0:T(8,128)(2,1)} collective-permute-done((bf16[768,768]{1,0:T(8,128)(2,1)}, bf16[768,768]{1,0:T(8,128)(2,1)}, u32[]{:S(2)}, u32[]{:S(2)}) %collective-permute-start.38) | collective-permute-done | bytes 1179680 | tf_op jit(solution)/shard_map/ppermute | solution.py:681
  392.0 56.3 %collective-permute-done.56 = f32[2,768]{1,0:T(2,128)S(1)} collective-permute-done((f32[2,768]{1,0:T(2,128)S(1)}, f32[2,768]{1,0:T(2,128)S(1)}, u32[]{:S(2)}, u32[]{:S(2)}) %collective-permute-start.56) | collective-permute-done | bytes 6176 | tf_op jit(solution)/shard_map/ppermute | solution.py:681
  457.4 2.7 collective-permute-start.59
  465.8 3.1 collective-permute-done.39
  471.9 9.6 %collective-permute-done.48 = bf16[384,768]{1,0:T(8,128)(2,1)} collective-permute-done((bf16[384,768]{1,0:T(8,128)(2,1)}, bf16[384,768]{1,0:T(8,128)(2,1)}, u32[]{:S(2)}, u32[]{:S(2)}) %collective-permute-start.48) | collective-permute-done | bytes 589856 | tf_op jit(solution)/shard_map/ppermute | solution.py:658
  484.6 2.9 collective-permute-done.22
  494.3 2.9 collective-permute-start.24
  497.6 2.9 collective-permute-start.50
  500.5 8.3 %collective-permute-done.24 = bf16[24,2304]{1,0:T(8,128)(2,1)S(1)} collective-permute-done((bf16[24,2304]{1,0:T(8,128)(2,1)S(1)}, bf16[24,2304]{1,0:T(8,128)(2,1)S(1)}, u32[]{:S(2)}, u32[]{:S(2)}) %collective-permute-start.24) | collective-permute-done | bytes 110624 | tf_op jit(solution)/shard_map/ppermute | solution.py:658
  509.0 2.9 collective-permute-done.41
  512.0 5.4 collective-permute-done.50
  517.5 2.3 collective-permute-done.25
  519.8 6.7 %collective-permute-start.26 = (bf16[48,2304]{1,0:T(8,128)(2,1)S(1)}, bf16[48,2304]{1,0:T(8,128)(2,1)S(1)}, u32[]{:S(2)}, u32[]{:S(2)}) collective-permute-start(bf16[48,2304]{1,0:T(8,128)(2,1)S(1)} %maximum_select_fusion.11), channel_id=1, source_target_pairs={{0,8},{4,12},{8,0},{12,4},{16,24},{20,28},{24,16},{28,20},{1,9},{5... | collective-permute-start | bytes 663560 | tf_op jit(solution)/shard_map/ppermute | solution.py:662
  528.6 2.5 collective-permute-done.51
  536.7 3.5 collective-permute-done.43
  541.3 4.3 collective-permute-done.52
  548.3 2.9 fusion
  555.4 3.6 reshape.145
  559.0 2.7 slice_bitcast_fusion.2
  561.7 2.9 fusion.2
  564.5 5.0 collective-permute-done.53
  569.5 2.9 fusion.3
  (238 shorter events, 104.0 us)
Async XLA Ops:
  17.0 5.7 collective-permute-start.4
  19.8 21.1 %collective-permute-start = (bf16[512,768]{1,0:T(8,128)(2,1)}, bf16[512,768]{1,0:T(8,128)(2,1)S(1)}, u32[]{:S(2)}, u32[]{:S(2)}) collective-permute-start(bf16[512,768]{1,0:T(8,128)(2,1)} %get-tuple-element.106), channel_id=1, source_target_pairs={{0,2},{2,0},{1,3},{3,1},{4,6},{6,4},{5,7},{7,5},{8,10},{10,8},{9,1... | collective-permute-start | bytes 2359304 | tf_op jit(solution)/shard_map/ppermute | solution.py:681
  23.7 46.3 %collective-permute-start.5 = (bf16[2,192,1152]{2,1,0:T(8,128)(2,1)}, bf16[2,192,1152]{2,1,0:T(8,128)(2,1)S(1)}, u32[]{:S(2)}, u32[]{:S(2)}) collective-permute-start(bf16[2,192,1152]{2,1,0:T(8,128)(2,1)} %pad_maximum_fusion.3), channel_id=1, source_target_pairs={{0,2},{2,0},{1,3},{3,1},{4,6},{6,4},{5,7},{7,5},{8,10},{10,8},{9,1... | collective-permute-start | bytes 2654216 | tf_op jit(solution)/shard_map/ppermute | solution.py:681
  23.7 44.9 %collective-permute-start.8 = (bf16[192,768]{1,0:T(8,128)(2,1)}, bf16[192,768]{1,0:T(8,128)(2,1)}, u32[]{:S(2)}, u32[]{:S(2)}) collective-permute-start(bf16[192,768]{1,0:T(8,128)(2,1)} %param.17), channel_id=1, source_target_pairs={{0,2},{2,0},{1,3},{3,1},{4,6},{6,4},{5,7},{7,5},{8,10},{10,8},{9,1... | collective-permute-start | bytes 884744 | tf_op jit(solution)/shard_map/ppermute | solution.py:681
  25.7 47.6 %collective-permute-start.2 = (bf16[512,768]{1,0:T(8,128)(2,1)S(1)}, bf16[512,768]{1,0:T(8,128)(2,1)}, u32[]{:S(2)}, u32[]{:S(2)}) collective-permute-start(bf16[512,768]{1,0:T(8,128)(2,1)S(1)} %get-tuple-element.107.x0.xo), channel_id=1, source_target_pairs={{0,1},{1,0},{2,3},{3,2},{4,5},{5,4},{6,7},{7,6},{8,9},{9,8},{10,11... | collective-permute-start | bytes 2359304 | tf_op jit(solution)/shard_map/ppermute | solution.py:677
  25.7 40.4 %collective-permute-start.6 = (bf16[3,3,192]{2,1,0:T(4,128)(2,1)S(1)}, bf16[3,3,192]{2,1,0:T(4,128)(2,1)S(1)}, u32[]{:S(2)}, u32[]{:S(2)}) collective-permute-start(bf16[3,3,192]{2,1,0:T(4,128)(2,1)S(1)} %copy-done.22), channel_id=1, source_target_pairs={{0,2},{2,0},{1,3},{3,1},{4,6},{6,4},{5,7},{7,5},{8,10},{10,8},{9,1... | collective-permute-start | bytes 10376 | tf_op jit(solution)/shard_map/ppermute | solution.py:681
  40.9 34.2 %collective-permute-start.3 = (bf16[512,768]{1,0:T(8,128)(2,1)S(1)}, bf16[512,768]{1,0:T(8,128)(2,1)}, u32[]{:S(2)}, u32[]{:S(2)}) collective-permute-start(bf16[512,768]{1,0:T(8,128)(2,1)S(1)} %collective-permute-done.x1.xx), channel_id=1, source_target_pairs={{0,1},{1,0},{2,3},{3,2},{4,5},{5,4},{6,7},{7,6},{8,9},{9,8},{10,11... | collective-permute-start | bytes 2359304 | tf_op jit(solution)/shard_map/ppermute | solution.py:677
  66.1 84.5 %collective-permute-start.10 = (bf16[768,768]{1,0:T(8,128)(2,1)}, bf16[768,768]{1,0:T(8,128)(2,1)}, u32[]{:S(2)}, u32[]{:S(2)}) collective-permute-start(bf16[768,768]{1,0:T(8,128)(2,1)} %wu.1), channel_id=1, source_target_pairs={{0,2},{2,0},{1,3},{3,1},{4,6},{6,4},{5,7},{7,5},{8,10},{10,8},{9,1... | collective-permute-start | bytes 3538952 | tf_op jit(solution)/shard_map/ppermute | solution.py:681
  68.6 92.5 %collective-permute-start.14 = (bf16[768,768]{1,0:T(8,128)(2,1)}, bf16[768,768]{1,0:T(8,128)(2,1)}, u32[]{:S(2)}, u32[]{:S(2)}) collective-permute-start(bf16[768,768]{1,0:T(8,128)(2,1)} %wu.1), channel_id=1, source_target_pairs={{0,1},{1,0},{2,3},{3,2},{4,5},{5,4},{6,7},{7,6},{8,9},{9,8},{10,11... | collective-permute-start | bytes 3538952 | tf_op jit(solution)/shard_map/ppermute | solution.py:677
  70.9 41.1 %collective-permute-start.1 = (bf16[512,768]{1,0:T(8,128)(2,1)}, bf16[512,768]{1,0:T(8,128)(2,1)S(1)}, u32[]{:S(2)}, u32[]{:S(2)}) collective-permute-start(bf16[512,768]{1,0:T(8,128)(2,1)} %get-tuple-element.104), channel_id=1, source_target_pairs={{0,2},{2,0},{1,3},{3,1},{4,6},{6,4},{5,7},{7,5},{8,10},{10,8},{9,1... | collective-permute-start | bytes 2359304 | tf_op jit(solution)/shard_map/ppermute | solution.py:681
  73.3 77.4 %collective-permute-start.11 = (bf16[768,768]{1,0:T(8,128)(2,1)}, bf16[768,768]{1,0:T(8,128)(2,1)}, u32[]{:S(2)}, u32[]{:S(2)}) collective-permute-start(bf16[768,768]{1,0:T(8,128)(2,1)} %wd.1), channel_id=1, source_target_pairs={{0,2},{2,0},{1,3},{3,1},{4,6},{6,4},{5,7},{7,5},{8,10},{10,8},{9,1... | collective-permute-start | bytes 3538952 | tf_op jit(solution)/shard_map/ppermute | solution.py:681
  75.1 86.0 %collective-permute-start.15 = (bf16[768,768]{1,0:T(8,128)(2,1)}, bf16[768,768]{1,0:T(8,128)(2,1)}, u32[]{:S(2)}, u32[]{:S(2)}) collective-permute-start(bf16[768,768]{1,0:T(8,128)(2,1)} %wd.1), channel_id=1, source_target_pairs={{0,1},{1,0},{2,3},{3,2},{4,5},{5,4},{6,7},{7,6},{8,9},{9,8},{10,11... | collective-permute-start | bytes 3538952 | tf_op jit(solution)/shard_map/ppermute | solution.py:677
  112.0 38.0 %collective-permute-start.9 = (bf16[384,768]{1,0:T(8,128)(2,1)S(1)}, bf16[384,768]{1,0:T(8,128)(2,1)S(1)}, u32[]{:S(2)}, u32[]{:S(2)}) collective-permute-start(bf16[384,768]{1,0:T(8,128)(2,1)S(1)} %bitcast.87), channel_id=1, source_target_pairs={{0,1},{1,0},{2,3},{3,2},{4,5},{5,4},{6,7},{7,6},{8,9},{9,8},{10,11... | collective-permute-start | bytes 1769480 | tf_op jit(solution)/shard_map/ppermute | solution.py:677
  150.6 25.6 %collective-permute-start.12 = (bf16[768,768]{1,0:T(8,128)(2,1)}, bf16[768,768]{1,0:T(8,128)(2,1)}, u32[]{:S(2)}, u32[]{:S(2)}) collective-permute-start(bf16[768,768]{1,0:T(8,128)(2,1)} %collective-permute-done.10.wu), channel_id=1, source_target_pairs={{0,1},{1,0},{2,3},{3,2},{4,5},{5,4},{6,7},{7,6},{8,9},{9,8},{10,11... | collective-permute-start | bytes 3538952 | tf_op jit(solution)/shard_map/ppermute | solution.py:677
  150.7 25.5 %collective-permute-start.13 = (bf16[768,768]{1,0:T(8,128)(2,1)}, bf16[768,768]{1,0:T(8,128)(2,1)}, u32[]{:S(2)}, u32[]{:S(2)}) collective-permute-start(bf16[768,768]{1,0:T(8,128)(2,1)} %collective-permute-done.11.wd), channel_id=1, source_target_pairs={{0,1},{1,0},{2,3},{3,2},{4,5},{5,4},{6,7},{7,6},{8,9},{9,8},{10,11... | collective-permute-start | bytes 3538952 | tf_op jit(solution)/shard_map/ppermute | solution.py:677
  236.1 85.0 %collective-permute-start.16 = (bf16[512,768]{1,0:T(8,128)(2,1)}, bf16[512,768]{1,0:T(8,128)(2,1)S(1)}, u32[]{:S(2)}, u32[]{:S(2)}) collective-permute-start(bf16[512,768]{1,0:T(8,128)(2,1)} %get-tuple-element.71), channel_id=1, source_target_pairs={{0,2},{2,0},{1,3},{3,1},{4,6},{6,4},{5,7},{7,5},{8,10},{10,8},{9,1... | collective-permute-start | bytes 2359304 | tf_op jit(solution)/shard_map/ppermute | solution.py:681
  237.9 110.5 %collective-permute-start.37 = (bf16[768,768]{1,0:T(8,128)(2,1)}, bf16[768,768]{1,0:T(8,128)(2,1)}, u32[]{:S(2)}, u32[]{:S(2)}) collective-permute-start(bf16[768,768]{1,0:T(8,128)(2,1)} %get-tuple-element.93), channel_id=1, source_target_pairs={{0,1},{1,0},{2,3},{3,2},{4,5},{5,4},{6,7},{7,6},{8,9},{9,8},{10,11... | collective-permute-start | bytes 3538952 | tf_op jit(solution)/shard_map/ppermute | solution.py:677
  238.0 136.3 %collective-permute-start.36 = (bf16[768,768]{1,0:T(8,128)(2,1)}, bf16[768,768]{1,0:T(8,128)(2,1)}, u32[]{:S(2)}, u32[]{:S(2)}) collective-permute-start(bf16[768,768]{1,0:T(8,128)(2,1)} %get-tuple-element.91), channel_id=1, source_target_pairs={{0,1},{1,0},{2,3},{3,2},{4,5},{5,4},{6,7},{7,6},{8,9},{9,8},{10,11... | collective-permute-start | bytes 3538952 | tf_op jit(solution)/shard_map/ppermute | solution.py:677
  238.4 115.0 %collective-permute-start.46 = (bf16[768,768]{1,0:T(8,128)(2,1)}, bf16[768,768]{1,0:T(8,128)(2,1)}, u32[]{:S(2)}, u32[]{:S(2)}) collective-permute-start(bf16[768,768]{1,0:T(8,128)(2,1)} %get-tuple-element.97), channel_id=1, source_target_pairs={{0,1},{1,0},{2,3},{3,2},{4,5},{5,4},{6,7},{7,6},{8,9},{9,8},{10,11... | collective-permute-start | bytes 3538952 | tf_op jit(solution)/shard_map/ppermute | solution.py:677
  240.4 81.3 %collective-permute-start.29 = (bf16[192,768]{1,0:T(8,128)(2,1)}, bf16[192,768]{1,0:T(8,128)(2,1)}, u32[]{:S(2)}, u32[]{:S(2)}) collective-permute-start(bf16[192,768]{1,0:T(8,128)(2,1)} %fusion.5), channel_id=1, source_target_pairs={{0,2},{2,0},{1,3},{3,1},{4,6},{6,4},{5,7},{7,5},{8,10},{10,8},{9,1... | collective-permute-start | bytes 884744 | tf_op jit(solution)/shard_map/ppermute | solution.py:681
  321.1 41.4 %collective-permute-start.18 = (bf16[1024,768]{1,0:T(8,128)(2,1)}, bf16[1024,768]{1,0:T(8,128)(2,1)S(1)}, u32[]{:S(2)}, u32[]{:S(2)}) collective-permute-start(bf16[1024,768]{1,0:T(8,128)(2,1)} %get-tuple-element.82), channel_id=1, source_target_pairs={{0,1},{1,0},{2,3},{3,2},{4,5},{5,4},{6,7},{7,6},{8,9},{9,8},{10,11... | collective-permute-start | bytes 4718600 | tf_op jit(solution)/shard_map/ppermute | solution.py:677
  322.8 5.9 %collective-permute-start.30 = (bf16[96,768]{1,0:T(8,128)(2,1)S(1)}, bf16[96,768]{1,0:T(8,128)(2,1)S(1)}, u32[]{:S(2)}, u32[]{:S(2)}) collective-permute-start(bf16[96,768]{1,0:T(8,128)(2,1)S(1)} %dynamic-slice_convert_fusion.9), channel_id=1, source_target_pairs={{0,4},{4,0},{8,12},{12,8},{16,20},{20,16},{24,28},{28,24},{1,5},{5... | collective-permute-start | bytes 442376 | tf_op jit(solution)/shard_map/ppermute | solution.py:658
  348.4 13.2 %collective-permute-start.20 = (bf16[2,192,1152]{2,1,0:T(8,128)(2,1)}, bf16[2,192,1152]{2,1,0:T(8,128)(2,1)S(1)}, u32[]{:S(2)}, u32[]{:S(2)}) collective-permute-start(bf16[2,192,1152]{2,1,0:T(8,128)(2,1)} %get-tuple-element.87), channel_id=1, source_target_pairs={{0,1},{1,0},{2,3},{3,2},{4,5},{5,4},{6,7},{7,6},{8,9},{9,8},{10,11... | collective-permute-start | bytes 2654216 | tf_op jit(solution)/shard_map/ppermute | solution.py:677
  353.1 100.5 %collective-permute-start.45 = (bf16[768,768]{1,0:T(8,128)(2,1)}, bf16[768,768]{1,0:T(8,128)(2,1)}, u32[]{:S(2)}, u32[]{:S(2)}) collective-permute-start(bf16[768,768]{1,0:T(8,128)(2,1)} %get-tuple-element.95), channel_id=1, source_target_pairs={{0,1},{1,0},{2,3},{3,2},{4,5},{5,4},{6,7},{7,6},{8,9},{9,8},{10,11... | collective-permute-start | bytes 3538952 | tf_op jit(solution)/shard_map/ppermute | solution.py:677
  353.4 6.2 %collective-permute-start.35 = (bf16[96,768]{1,0:T(8,128)(2,1)S(1)}, bf16[96,768]{1,0:T(8,128)(2,1)S(1)}, u32[]{:S(2)}, u32[]{:S(2)}) collective-permute-start(bf16[96,768]{1,0:T(8,128)(2,1)S(1)} %maximum_select_fusion.12), channel_id=1, source_target_pairs={{0,4},{4,0},{8,12},{12,8},{16,20},{20,16},{24,28},{28,24},{1,5},{5... | collective-permute-start | bytes 442376 | tf_op jit(solution)/shard_map/ppermute | solution.py:662
  359.5 29.2 %collective-permute-start.38 = (bf16[768,768]{1,0:T(8,128)(2,1)}, bf16[768,768]{1,0:T(8,128)(2,1)}, u32[]{:S(2)}, u32[]{:S(2)}) collective-permute-start(bf16[768,768]{1,0:T(8,128)(2,1)} %add_convert_fusion.1), channel_id=1, source_target_pairs={{0,2},{2,0},{1,3},{3,1},{4,6},{6,4},{5,7},{7,5},{8,10},{10,8},{9,1... | collective-permute-start | bytes 3538952 | tf_op jit(solution)/shard_map/ppermute | solution.py:681
  361.5 93.5 %collective-permute-start.47 = (bf16[768,768]{1,0:T(8,128)(2,1)}, bf16[768,768]{1,0:T(8,128)(2,1)}, u32[]{:S(2)}, u32[]{:S(2)}) collective-permute-start(bf16[768,768]{1,0:T(8,128)(2,1)} %add_convert_fusion), channel_id=1, source_target_pairs={{0,2},{2,0},{1,3},{3,1},{4,6},{6,4},{5,7},{7,5},{8,10},{10,8},{9,1... | collective-permute-start | bytes 3538952 | tf_op jit(solution)/shard_map/ppermute | solution.py:681
  373.1 90.4 %collective-permute-start.21 = (bf16[192,2304]{1,0:T(8,128)(2,1)}, bf16[192,2304]{1,0:T(8,128)(2,1)S(1)}, u32[]{:S(2)}, u32[]{:S(2)}) collective-permute-start(bf16[192,2304]{1,0:T(8,128)(2,1)} %slice_bitcast_fusion), channel_id=1, source_target_pairs={{0,2},{2,0},{1,3},{3,1},{4,6},{6,4},{5,7},{7,5},{8,10},{10,8},{9,1... | collective-permute-start | bytes 2654216 | tf_op jit(solution)/shard_map/ppermute | solution.py:681
  374.3 115.3 %collective-permute-start.19 = (bf16[512,768]{1,0:T(8,128)(2,1)}, bf16[512,768]{1,0:T(8,128)(2,1)}, u32[]{:S(2)}, u32[]{:S(2)}) collective-permute-start(bf16[512,768]{1,0:T(8,128)(2,1)} %get-tuple-element.85), channel_id=1, source_target_pairs={{0,2},{2,0},{1,3},{3,1},{4,6},{6,4},{5,7},{7,5},{8,10},{10,8},{9,1... | collective-permute-start | bytes 2359304 | tf_op jit(solution)/shard_map/ppermute | solution.py:681
  388.7 59.7 %collective-permute-start.56 = (f32[2,768]{1,0:T(2,128)S(1)}, f32[2,768]{1,0:T(2,128)S(1)}, u32[]{:S(2)}, u32[]{:S(2)}) collective-permute-start(f32[2,768]{1,0:T(2,128)S(1)} %fusion.8), channel_id=1, source_target_pairs={{0,2},{2,0},{1,3},{3,1},{4,6},{6,4},{5,7},{7,5},{8,10},{10,8},{9,1... | collective-permute-start | bytes 18440 | tf_op jit(solution)/shard_map/ppermute | solution.py:681
  452.3 16.6 %collective-permute-start.39 = (bf16[384,768]{1,0:T(8,128)(2,1)}, bf16[384,768]{1,0:T(8,128)(2,1)}, u32[]{:S(2)}, u32[]{:S(2)}) collective-permute-start(bf16[384,768]{1,0:T(8,128)(2,1)} %dynamic-slice_convert_fusion.1), channel_id=1, source_target_pairs={{0,4},{4,0},{8,12},{12,8},{16,20},{20,16},{24,28},{28,24},{1,5},{5... | collective-permute-start | bytes 1769480 | tf_op jit(solution)/shard_map/ppermute | solution.py:658
  461.0 20.5 %collective-permute-start.48 = (bf16[384,768]{1,0:T(8,128)(2,1)}, bf16[384,768]{1,0:T(8,128)(2,1)}, u32[]{:S(2)}, u32[]{:S(2)}) collective-permute-start(bf16[384,768]{1,0:T(8,128)(2,1)} %dynamic-slice_convert_fusion), channel_id=1, source_target_pairs={{0,4},{4,0},{8,12},{12,8},{16,20},{20,16},{24,28},{28,24},{1,5},{5... | collective-permute-start | bytes 1769480 | tf_op jit(solution)/shard_map/ppermute | solution.py:658
  464.9 22.6 %collective-permute-start.22 = (bf16[96,2304]{1,0:T(8,128)(2,1)S(1)}, bf16[96,2304]{1,0:T(8,128)(2,1)S(1)}, u32[]{:S(2)}, u32[]{:S(2)}) collective-permute-start(bf16[96,2304]{1,0:T(8,128)(2,1)S(1)} %dynamic-slice_convert_fusion.2), channel_id=1, source_target_pairs={{0,4},{4,0},{8,12},{12,8},{16,20},{20,16},{24,28},{28,24},{1,5},{5... | collective-permute-start | bytes 1327112 | tf_op jit(solution)/shard_map/ppermute | solution.py:658
  470.1 27.2 %collective-permute-start.40 = (bf16[192,768]{1,0:T(8,128)(2,1)S(1)}, bf16[192,768]{1,0:T(8,128)(2,1)S(1)}, u32[]{:S(2)}, u32[]{:S(2)}) collective-permute-start(bf16[192,768]{1,0:T(8,128)(2,1)S(1)} %dynamic-slice_convert_fusion.4), channel_id=1, source_target_pairs={{0,8},{4,12},{8,0},{12,4},{16,24},{20,28},{24,16},{28,20},{1,9},{5... | collective-permute-start | bytes 884744 | tf_op jit(solution)/shard_map/ppermute | solution.py:658
  482.7 14.8 %collective-permute-start.49 = (bf16[192,768]{1,0:T(8,128)(2,1)S(1)}, bf16[192,768]{1,0:T(8,128)(2,1)S(1)}, u32[]{:S(2)}, u32[]{:S(2)}) collective-permute-start(bf16[192,768]{1,0:T(8,128)(2,1)S(1)} %dynamic-slice_convert_fusion.3), channel_id=1, source_target_pairs={{0,8},{4,12},{8,0},{12,4},{16,24},{20,28},{24,16},{28,20},{1,9},{5... | collective-permute-start | bytes 884744 | tf_op jit(solution)/shard_map/ppermute | solution.py:658
  487.6 6.6 %collective-permute-start.23 = (bf16[48,2304]{1,0:T(8,128)(2,1)S(1)}, bf16[48,2304]{1,0:T(8,128)(2,1)S(1)}, u32[]{:S(2)}, u32[]{:S(2)}) collective-permute-start(bf16[48,2304]{1,0:T(8,128)(2,1)S(1)} %dynamic-slice_convert_fusion.6), channel_id=1, source_target_pairs={{0,8},{4,12},{8,0},{12,4},{16,24},{20,28},{24,16},{28,20},{1,9},{5... | collective-permute-start | bytes 663560 | tf_op jit(solution)/shard_map/ppermute | solution.py:658
  494.3 14.4 %collective-permute-start.24 = (bf16[24,2304]{1,0:T(8,128)(2,1)S(1)}, bf16[24,2304]{1,0:T(8,128)(2,1)S(1)}, u32[]{:S(2)}, u32[]{:S(2)}) collective-permute-start(bf16[24,2304]{1,0:T(8,128)(2,1)S(1)} %dynamic-slice_convert_fusion.10), channel_id=1, source_target_pairs={{0,16},{4,20},{8,24},{12,28},{16,0},{20,4},{24,8},{28,12},{1,17},{... | collective-permute-start | bytes 331784 | tf_op jit(solution)/shard_map/ppermute | solution.py:658
  497.3 14.6 %collective-permute-start.41 = (bf16[96,768]{1,0:T(8,128)(2,1)S(1)}, bf16[96,768]{1,0:T(8,128)(2,1)S(1)}, u32[]{:S(2)}, u32[]{:S(2)}) collective-permute-start(bf16[96,768]{1,0:T(8,128)(2,1)S(1)} %dynamic-slice_convert_fusion.8), channel_id=1, source_target_pairs={{0,16},{4,20},{8,24},{12,28},{16,0},{20,4},{24,8},{28,12},{1,17},{... | collective-permute-start | bytes 442376 | tf_op jit(solution)/shard_map/ppermute | solution.py:658
  497.6 19.8 %collective-permute-start.50 = (bf16[96,768]{1,0:T(8,128)(2,1)S(1)}, bf16[96,768]{1,0:T(8,128)(2,1)S(1)}, u32[]{:S(2)}, u32[]{:S(2)}) collective-permute-start(bf16[96,768]{1,0:T(8,128)(2,1)S(1)} %dynamic-slice_convert_fusion.7), channel_id=1, source_target_pairs={{0,16},{4,20},{8,24},{12,28},{16,0},{20,4},{24,8},{28,12},{1,17},{... | collective-permute-start | bytes 442376 | tf_op jit(solution)/shard_map/ppermute | solution.py:658
  508.9 10.9 %collective-permute-start.25 = (bf16[24,2304]{1,0:T(8,128)(2,1)S(1)}, bf16[24,2304]{1,0:T(8,128)(2,1)S(1)}, u32[]{:S(2)}, u32[]{:S(2)}) collective-permute-start(bf16[24,2304]{1,0:T(8,128)(2,1)S(1)} %add_convert_fusion.4), channel_id=1, source_target_pairs={{0,16},{4,20},{8,24},{12,28},{16,0},{20,4},{24,8},{28,12},{1,17},{... | collective-permute-start | bytes 331784 | tf_op jit(solution)/shard_map/ppermute | solution.py:662
  511.9 15.5 %collective-permute-start.42 = (bf16[96,768]{1,0:T(8,128)(2,1)S(1)}, bf16[96,768]{1,0:T(8,128)(2,1)S(1)}, u32[]{:S(2)}, u32[]{:S(2)}) collective-permute-start(bf16[96,768]{1,0:T(8,128)(2,1)S(1)} %add_convert_fusion.3), channel_id=1, source_target_pairs={{0,16},{4,20},{8,24},{12,28},{16,0},{20,4},{24,8},{28,12},{1,17},{... | collective-permute-start | bytes 442376 | tf_op jit(solution)/shard_map/ppermute | solution.py:662
  517.5 13.6 %collective-permute-start.51 = (bf16[96,768]{1,0:T(8,128)(2,1)S(1)}, bf16[96,768]{1,0:T(8,128)(2,1)S(1)}, u32[]{:S(2)}, u32[]{:S(2)}) collective-permute-start(bf16[96,768]{1,0:T(8,128)(2,1)S(1)} %add_convert_fusion.2), channel_id=1, source_target_pairs={{0,16},{4,20},{8,24},{12,28},{16,0},{20,4},{24,8},{28,12},{1,17},{... | collective-permute-start | bytes 442376 | tf_op jit(solution)/shard_map/ppermute | solution.py:662
  519.8 14.1 %collective-permute-start.26 = (bf16[48,2304]{1,0:T(8,128)(2,1)S(1)}, bf16[48,2304]{1,0:T(8,128)(2,1)S(1)}, u32[]{:S(2)}, u32[]{:S(2)}) collective-permute-start(bf16[48,2304]{1,0:T(8,128)(2,1)S(1)} %maximum_select_fusion.11), channel_id=1, source_target_pairs={{0,8},{4,12},{8,0},{12,4},{16,24},{20,28},{24,16},{28,20},{1,9},{5... | collective-permute-start | bytes 663560 | tf_op jit(solution)/shard_map/ppermute | solution.py:662
  527.5 12.7 %collective-permute-start.43 = (bf16[192,768]{1,0:T(8,128)(2,1)S(1)}, bf16[192,768]{1,0:T(8,128)(2,1)S(1)}, u32[]{:S(2)}, u32[]{:S(2)}) collective-permute-start(bf16[192,768]{1,0:T(8,128)(2,1)S(1)} %maximum_select_fusion.9), channel_id=1, source_target_pairs={{0,8},{4,12},{8,0},{12,4},{16,24},{20,28},{24,16},{28,20},{1,9},{5... | collective-permute-start | bytes 884744 | tf_op jit(solution)/shard_map/ppermute | solution.py:662
  531.1 14.5 %collective-permute-start.52 = (bf16[192,768]{1,0:T(8,128)(2,1)S(1)}, bf16[192,768]{1,0:T(8,128)(2,1)}, u32[]{:S(2)}, u32[]{:S(2)}) collective-permute-start(bf16[192,768]{1,0:T(8,128)(2,1)S(1)} %maximum_select_fusion.10), channel_id=1, source_target_pairs={{0,8},{4,12},{8,0},{12,4},{16,24},{20,28},{24,16},{28,20},{1,9},{5... | collective-permute-start | bytes 884744 | tf_op jit(solution)/shard_map/ppermute | solution.py:662
  534.0 13.8 %collective-permute-start.27 = (bf16[96,2304]{1,0:T(8,128)(2,1)S(1)}, bf16[96,2304]{1,0:T(8,128)(2,1)S(1)}, u32[]{:S(2)}, u32[]{:S(2)}) collective-permute-start(bf16[96,2304]{1,0:T(8,128)(2,1)S(1)} %maximum_select_fusion.7), channel_id=1, source_target_pairs={{0,4},{4,0},{8,12},{12,8},{16,20},{20,16},{24,28},{28,24},{1,5},{5... | collective-permute-start | bytes 1327112 | tf_op jit(solution)/shard_map/ppermute | solution.py:662
  540.4 21.3 %collective-permute-start.44 = (bf16[384,768]{1,0:T(8,128)(2,1)S(1)}, bf16[384,768]{1,0:T(8,128)(2,1)}, u32[]{:S(2)}, u32[]{:S(2)}) collective-permute-start(bf16[384,768]{1,0:T(8,128)(2,1)S(1)} %maximum_select_fusion.5), channel_id=1, source_target_pairs={{0,4},{4,0},{8,12},{12,8},{16,20},{20,16},{24,28},{28,24},{1,5},{5... | collective-permute-start | bytes 1769480 | tf_op jit(solution)/shard_map/ppermute | solution.py:662
  546.8 22.7 %collective-permute-start.53 = (bf16[384,768]{1,0:T(8,128)(2,1)S(1)}, bf16[384,768]{1,0:T(8,128)(2,1)}, u32[]{:S(2)}, u32[]{:S(2)}) collective-permute-start(bf16[384,768]{1,0:T(8,128)(2,1)S(1)} %maximum_select_fusion.6), channel_id=1, source_target_pairs={{0,4},{4,0},{8,12},{12,8},{16,20},{20,16},{24,28},{28,24},{1,5},{5... | collective-permute-start | bytes 1769480 | tf_op jit(solution)/shard_map/ppermute | solution.py:662
  (39 other events, 377.1 us)
